TPU v7x, 512 devices: a whole 4x4x16 slice. The times are simulated.
512 devices in a mesh: seq: 16 (over x, y_hi, core), batch: 32 (over z, y_lo).
Axes of the slice: x: 4, y: 4 (y_hi: 2, y_lo: 2; y = y_hi * 2 + y_lo), z: 16, core: 2. Of those that a mesh axis runs over, the one named last changes fastest.
Arguments:
- hidden: bfloat16 [65536, 512], P(('batch', 'seq')), parts along dimension 0, may hold values from -500 to 500
- norm_gain: float32 [512], replicated, may hold values from 0.5 to 1.5
- input_weight: bfloat16 [512, 2176], replicated, may hold values from -0.25 to 0.25
- step_weight: bfloat16 [512, 16], replicated, may hold values from -1 to 1
- conv_weight: float32 [4, 1152], replicated, may hold values from -3 to 3
- conv_bias: float32 [1152], replicated, may hold values from -3 to 3
- step_bias: float32 [16], replicated, may hold values from -11 to 1
- log_rate: float32 [16], replicated, may hold values from -3 to 6
- skip_gain: float32 [16], replicated, may hold values from 0.5 to 1.5
- gate_gain: float32 [1024], replicated, may hold values from 0.5 to 1.5
- output_weight: bfloat16 [1024, 512], replicated, may hold values from -0.1875 to 0.1875
Outputs:
- mixed: bfloat16 [65536, 512], P(('batch', 'seq')), parts along dimension 0
There are 32 independent parts, one for each index of `batch`. A program takes and returns all parts, laid end to end along the dimension named above; an argument that names none is the same for every part. Nothing has to cross between parts.
All inputs are finite; a program needn't handle non-finite values.
Results may differ from a plain program's by a relative error of at most 0.0078.
Values may be sent and summed in bfloat16 or wider, within the bound.
A program may use at most 128 MiB of HBM per device.

v0:
```python
import jax
import jax.numpy as jnp
from jax import lax
from jax.sharding import PartitionSpec as P

E = 1024
N = 64
P_SIZE = 64
K = 4
BLOCK = 128
HEADS = 16


eps = 1e-05


def extended_2(cells, sides, width):
    for axis, dim in sides:
        count = lax.axis_size(axis)
        ends = count - 1
        head = lax.slice_in_dim(cells, 0, width, axis=dim)
        tail = lax.slice_in_dim(cells, cells.shape[dim] - width, cells.shape[dim], axis=dim)
        cells = jnp.concatenate(
            [
                lax.ppermute(tail, axis, [(i, (i + 1) % count) for i in range(ends)]),
                cells,
                lax.ppermute(head, axis, [((i + 1) % count, i) for i in range(ends)]),
            ],
            axis=dim,
        )
    return cells


def prefix(shard, axis, combine, identity):
    count, index = (lax.axis_size(axis), lax.axis_index(axis))
    everything = jax.tree.map(
        lambda part, kind: lax.all_gather(part.astype(kind), axis),
        shard,
        (jnp.bfloat16, jnp.bfloat16),
    )
    start = jax.tree.map(
        lambda part, zero: jnp.broadcast_to(jnp.asarray(zero, part.dtype), part.shape),
        shard,
        identity,
    )

    def turn(k, before):
        reached = k < index
        new = combine(
            before, jax.tree.map(lambda part, own: part[k].astype(own.dtype), everything, shard)
        )
        return jax.tree.map(lambda a, b: jnp.where(reached, a, b), new, before)

    return lax.fori_loop(0, count, turn, start)


def prefix_2(shard, axis, combine, identity):
    count, index = (lax.axis_size(axis), lax.axis_index(axis))
    everything = jax.tree.map(lambda part: lax.all_gather(part, axis), shard)
    start = jax.tree.map(
        lambda part, zero: jnp.broadcast_to(jnp.asarray(zero, part.dtype), part.shape),
        shard,
        identity,
    )

    def turn(k, before):
        at = count - 1 - k
        reached = at > index
        new = combine(before, jax.tree.map(lambda part: part[at], everything))
        return jax.tree.map(lambda a, b: jnp.where(reached, a, b), new, before)

    return lax.fori_loop(0, count, turn, start)


def normed(entry_matrix, gain):
    floats = entry_matrix.astype(jnp.float32)
    scale = lax.rsqrt(jnp.mean(floats * floats, axis=-1, keepdims=True) + eps)
    return (floats * scale * gain).astype(jnp.bfloat16)


def project(stacked, norm_gain, input_weight, step_weight):
    chains, length_rows, feature_count = stacked.shape
    normal_rows = normed(stacked.reshape(chains * length_rows, feature_count), norm_gain)
    projected = jnp.dot(normal_rows, input_weight, preferred_element_type=jnp.float32).astype(
        jnp.bfloat16
    )
    step_raw = jnp.dot(normal_rows, step_weight, preferred_element_type=jnp.float32)
    return (projected.reshape(chains, length_rows, -1), step_raw.reshape(chains, length_rows, -1))


def block_step(carry, pieces):
    memory, running = carry
    signal, writer, reader, log_decay = pieces
    cumulated = jnp.cumsum(log_decay, axis=0)
    per_head = cumulated.T
    spread = per_head[:, :, None] - per_head[:, None, :]
    causal = lax.broadcasted_iota(jnp.int32, (BLOCK, BLOCK), 0) >= lax.broadcasted_iota(
        jnp.int32, (BLOCK, BLOCK), 1
    )
    decay = jnp.where(causal[None], jnp.exp(jnp.where(causal[None], spread, 0.0)), 0.0)
    scores = jnp.dot(reader, writer.T, preferred_element_type=jnp.float32)
    weights = (decay * scores[None]).astype(jnp.bfloat16)
    heads_x = signal.reshape(BLOCK, HEADS, P_SIZE)
    inside = jnp.einsum("hts,shp->thp", weights, heads_x, preferred_element_type=jnp.float32)
    carried = jnp.einsum(
        "tn,hnp->thp", reader.astype(jnp.float32), memory, precision=lax.Precision.HIGHEST
    )
    result = inside + jnp.exp(cumulated)[:, :, None] * carried
    decay_tail = jnp.exp(cumulated[-1][None, :] - cumulated)
    decayed = (decay_tail[:, :, None] * heads_x.astype(jnp.float32)).astype(jnp.bfloat16)
    renewed = jnp.exp(cumulated[-1])[:, None, None] * memory + jnp.einsum(
        "sn,shp->hnp", writer, decayed, preferred_element_type=jnp.float32
    )
    return (
        (renewed, running + cumulated[-1]),
        (result.reshape(BLOCK, E), running[None, :] + cumulated),
    )


def run_chain(projected, step_raw, rim, conv_weight, conv_bias, step_bias, log_rate):
    row_count = projected.shape[0]
    extended = jnp.concatenate([rim, projected[:, E:]], axis=0)
    filtered = conv_bias[None, :]
    for tap_index in range(K):
        filtered = filtered + conv_weight[tap_index][None, :] * extended[
            tap_index : tap_index + row_count
        ].astype(jnp.float32)
    activated = jax.nn.silu(filtered).astype(jnp.bfloat16)
    signal = activated[:, :E]
    writer = activated[:, E : E + N]
    reader = activated[:, E + N :]
    log_decay = -jnp.exp(log_rate)[None, :] * jax.nn.softplus(step_raw + step_bias[None, :])
    blocks = row_count // BLOCK
    start = (jnp.zeros((HEADS, N, P_SIZE), jnp.float32), jnp.zeros((HEADS,), jnp.float32))
    (memory, running), (inside, cumulated) = lax.scan(
        block_step,
        start,
        (
            signal.reshape(blocks, BLOCK, E),
            writer.reshape(blocks, BLOCK, N),
            reader.reshape(blocks, BLOCK, N),
            log_decay.reshape(blocks, BLOCK, HEADS),
        ),
    )
    return (
        signal,
        reader,
        projected[:, :E],
        inside.reshape(row_count, E),
        cumulated.reshape(row_count, HEADS),
        memory,
        running,
    )


def finish(
    signal, reader, gate_rows, inside, cumulated, incoming, skip_gain, gate_gain, output_weight
):
    row_count = signal.shape[0]
    carried = jnp.einsum(
        "tn,hnp->thp", reader.astype(jnp.float32), incoming, precision=lax.Precision.HIGHEST
    )
    output_rows = inside + (jnp.exp(cumulated)[:, :, None] * carried).reshape(row_count, E)
    gated = (
        output_rows + jnp.repeat(skip_gain, P_SIZE)[None, :] * signal.astype(jnp.float32)
    ) * jax.nn.silu(gate_rows.astype(jnp.float32))
    return jnp.dot(normed(gated, gate_gain), output_weight, preferred_element_type=jnp.float32)


def chain_join(earlier, later):
    log_early, state_early = earlier
    log_late, state_late = later
    return (log_early + log_late, jnp.exp(log_late)[:, :, None, None] * state_early + state_late)


def on_device(
    hidden,
    norm_gain,
    input_weight,
    step_weight,
    conv_weight,
    conv_bias,
    step_bias,
    log_rate,
    skip_gain,
    gate_gain,
    output_weight,
):

    def chain_local(projected, step_raw, rim):
        return run_chain(projected, step_raw, rim, conv_weight, conv_bias, step_bias, log_rate)

    def finish_local(signal, reader, gate_rows, inside, cumulated, incoming):
        return finish(
            signal,
            reader,
            gate_rows,
            inside,
            cumulated,
            incoming,
            skip_gain,
            gate_gain,
            output_weight,
        )

    def empty_states(chains):
        return (
            jnp.zeros((chains, HEADS), jnp.float32),
            jnp.zeros((chains, HEADS, N, P_SIZE), jnp.float32),
        )

    stacked = jnp.stack([hidden, hidden[:, ::-1]])
    projected, step_raw = project(stacked, norm_gain, input_weight, step_weight)
    padded = extended_2(projected[:, :, E:], (("seq", 1),), K - 1)
    left_rims = padded[:, : K - 1]
    right_rims = padded[:, -(K - 1) :][:, ::-1]
    forward_pieces = jax.vmap(chain_local)(projected, step_raw, left_rims)
    reverse_pieces = jax.vmap(chain_local)(projected[:, ::-1], step_raw[:, ::-1], right_rims)
    forward_in = prefix((forward_pieces[6], forward_pieces[5]), "seq", chain_join, empty_states(2))
    reverse_in = prefix_2(
        (reverse_pieces[6], reverse_pieces[5]), "seq", chain_join, empty_states(2)
    )
    forward_out = jax.vmap(finish_local)(
        forward_pieces[0],
        forward_pieces[1],
        forward_pieces[2],
        forward_pieces[3],
        forward_pieces[4],
        forward_in[1],
    )
    reverse_out = jax.vmap(finish_local)(
        reverse_pieces[0],
        reverse_pieces[1],
        reverse_pieces[2],
        reverse_pieces[3],
        reverse_pieces[4],
        reverse_in[1],
    )
    forward_part = forward_out[0] + forward_out[1][:, ::-1]
    backward_part = (reverse_out[0] + reverse_out[1][:, ::-1])[::-1].astype(jnp.bfloat16)
    backward_part = lax.optimization_barrier(backward_part)
    return (forward_part + backward_part.astype(jnp.float32)).astype(jnp.bfloat16)


def solution(mesh):
    in_specs = (P(("batch", "seq"), None), P(), P(), P(), P(), P(), P(), P(), P(), P(), P())
    out_specs = P(("batch", "seq"), None)
    return jax.shard_map(
        on_device, mesh=mesh, in_specs=in_specs, out_specs=out_specs, check_vma=False
    )
```

profile of v0, /device:TPU:1, one launch (start us, length us, event | category | flops | bytes accessed | tf_op | source)
XLA Modules:
  0.0 331.2 jit_solution(7804601432332821896)
XLA Ops:
  12.3 8.7 %collective-permute-start.1 = (bf16[2,3,1152]{2,0,1:T(2,128)(2,1)}, bf16[2,3,1152]{2,0,1:T(2,128)(2,1)}, u32[]{:S(2)}, u32[]{:S(2)}) collective-permute-start(bf16[2,3,1152]{2,0,1:T(2,128)(2,1)} %copy.82), channel_id=1, source_target_pairs={{32,0},{64,32},{96,64},{128,96},{160,128},{192,160},{224,192},{256... | collective-permute-start | bytes 41480 | tf_op jit(solution)/shard_map/ppermute | solution.py:27
  31.1 6.3 %slice.116 = bf16[2,128,1152]{1,2,0:T(8,128)(2,1)} reverse(bf16[2,128,1152]{1,2,0:T(8,128)(2,1)S(1)} %copy.80), dimensions={1} | reverse | bytes 1179648 | tf_op jit(solution)/shard_map/vmap()/slice | solution.py:122
  39.1 6.3 %rev.21 = bf16[2,3,1152]{1,2,0:T(8,128)(2,1)} reverse(bf16[2,3,1152]{1,2,0:T(8,128)(2,1)S(1)} %copy.65), dimensions={1} | reverse | bytes 27648 | tf_op jit(solution)/shard_map/rev | solution.py:216
  47.2 5.5 %multiply_convert_fusion.2 = (bf16[2,128,1152]{1,2,0:T(8,128)(2,1)S(1)}, bf16[2,128,1152]{1,2,0:T(8,128)(2,1)S(1)}) fusion(bf16[2,128,1152]{1,2,0:T(8,128)(2,1)} %slice.116, bf16[2,3,1152]{1,2,0:T(8,128)(2,1)} %rev.21, f32[1152]{0:T(1024)} %get-tuple-element.345, f32[1152]{0:T(1024)} %get-tuple-element.346, f32[1152]{0:T(1024)} %get-tuple-element.344, ...), kind=kLoop, calls=%fused_computation.32 | loop fusion | flops 15335424 | bytes 2409984 | tf_op jit(solution)/shard_map/vmap()/convert_element_type | solution.py:128
  54.8 2.0 copy.60
  60.1 2.6 copy.71
  67.2 8.6 %slice.124 = bf16[2,128,1024]{1,2,0:T(8,128)(2,1)} reverse(bf16[2,128,1024]{1,2,0:T(8,128)(2,1)} %copy.81), dimensions={1} | reverse | bytes 1048576 | tf_op jit(solution)/shard_map/vmap()/slice | solution.py:148
  78.2 20.2 %all-gather = bf16[32,1,16]{2,1,0:T(2,128)(2,1)S(1)} all-gather(bf16[2,1,16]{2,1,0:T(2,128)(2,1)} %slice.226), channel_id=2, replica_groups=mesh['seq'=16,'batch'=32] {'seq'}, dimensions={0}, use_global_device_ids=true | all-gather | bytes 1088 | tf_op jit(solution)/shard_map/all_gather | solution.py:37
  101.2 23.7 %all-gather.2 = f32[32,1,16]{2,1,0:T(1,128)} all-gather(f32[2,1,16]{2,1,0:T(1,128)S(1)} %slice.148), channel_id=4, replica_groups=mesh['seq'=16,'batch'=32] {'seq'}, dimensions={0}, use_global_device_ids=true | all-gather | bytes 2176 | tf_op jit(solution)/shard_map/all_gather | solution.py:59
  127.5 2.3 fusion.35
  129.9 2.5 fusion.62
  132.4 15.3 %all-gather.7.cloned.1.call-done = bf16[32,16,64,64]{3,2,1,0:T(8,128)(2,1)} async-done(((bf16[2,16,64,64]{3,2,1,0:T(8,128)(2,1)}), bf16[32,16,64,64]{3,2,1,0:T(8,128)(2,1)}) %all-gather.7.cloned.1.call-update) | async-done | bytes 4194320 | tf_op jit(solution)/shard_map/all_gather | solution.py:37
  147.7 51.2 %while.20 = (s32[]{:T(128)}, f32[2,16,64,64]{3,2,1,0:T(8,128)}, s32[]{:T(128)}, bf16[16,2,16]{2,1,0:T(2,128)(2,1)}, bf16[16,2,16,64,64]{4,3,2,1,0:T(8,128)(2,1)}, /*index=5*/s32[]{:T(128)}, s32[]{:T(128)}) while((s32[]{:T(128)}, f32[2,16,64,64]{3,2,1,0:T(8,128)}, s32[]{:T(128)}, bf16[16,2,16]{2,1,0:T(2,128)(2,1)}, ...), condition=%wide.region_3.4_spmd.clone, body=%wide.region_2.3_spmd.clone.sunk | while | flops 655396 | bytes 1311153 | solution.py:54
  148.3 2.3 fusion.91
  151.1 2.6 fusion.91
  154.3 2.6 fusion.91
  157.5 2.6 fusion.91
  160.8 2.6 fusion.91
  164.0 2.6 fusion.91
  167.2 2.6 fusion.91
  170.5 2.6 fusion.91
  173.7 2.6 fusion.91
  176.9 2.6 fusion.91
  180.1 2.6 fusion.91
  183.3 2.6 fusion.91
  186.5 2.6 fusion.91
  189.8 2.6 fusion.91
  193.0 2.6 fusion.91
  196.3 2.6 fusion.91
  198.9 2.6 copy.61
  205.4 68.6 %all-gather.9.cloned.1.call-done = f32[32,16,64,64]{3,2,1,0:T(8,128)} async-done(((f32[2,16,64,64]{3,2,1,0:T(8,128)}), f32[32,16,64,64]{3,2,1,0:T(8,128)}) %all-gather.9.cloned.1.call-update) | async-done | bytes 8388624 | tf_op jit(solution)/shard_map/all_gather | solution.py:59
  274.1 34.4 %while.21 = (s32[]{:T(128)}, f32[2,16,64,64]{3,2,1,0:T(8,128)S(1)}, s32[]{:T(128)}, f32[16,2,16]{2,1,0:T(2,128)}, f32[16,2,16,64,64]{4,3,2,1,0:T(8,128)}, /*index=5*/s32[]{:T(128)}, s32[]{:T(128)}, s32[]{:T(128)}, s32[]{:T(128)}) while((s32[]{:T(128)}, f32[2,16,64,64]{3,2,1,0:T(8,128)S(1)}, s32[]{:T(128)}, f32[16,2,16]{2,1,0:T(2,128)}, ...), condition=%wide.region_7.8_spmd.clone, body=%wide.region_6.7_spmd.clone.sunk | while | flops 524296 | bytes 1573423 | solution.py:72
  (191 shorter events, 100.8 us)
Async XLA Ops:
  6.5 4.1 %copy-start = (bf16[512,2176]{1,0:T(8,128)(2,1)S(1)}, bf16[512,2176]{1,0:T(8,128)(2,1)}, u32[]{:S(2)}) copy-start(bf16[512,2176]{1,0:T(8,128)(2,1)} %param.17) | copy-start | bytes 6684676
  6.5 4.0 %copy-start.29 = (f32[512]{0:T(512)S(1)}, f32[512]{0:T(512)}, u32[]{:S(2)}) copy-start(f32[512]{0:T(512)} %param.16) | copy-start | bytes 6148
  6.5 141.1 %all-gather.7.cloned.1.call-start = ((), (), s32[]{:S(2)}) async-start(), calls=%async_computation | async-start | bytes 8912896 | tf_op jit(solution)/shard_map/all_gather | solution.py:37
  10.6 12.9 %copy-start.14 = (bf16[128,512]{1,0:T(8,128)(2,1)S(1)}, bf16[128,512]{1,0:T(8,128)(2,1)}, u32[]{:S(2)}) copy-start(bf16[128,512]{1,0:T(8,128)(2,1)} %param.15) | copy-start | bytes 393220
  10.7 12.9 %copy-start.33 = (bf16[512,16]{0,1:T(8,128)(2,1)S(1)}, bf16[512,16]{0,1:T(8,128)(2,1)}, u32[]{:S(2)}) copy-start(bf16[512,16]{0,1:T(8,128)(2,1)} %param.18) | copy-start | bytes 49156
  10.7 13.2 %copy-start.34 = (f32[16]{0:T(128)S(1)}, f32[16]{0:T(128)}, u32[]{:S(2)}) copy-start(f32[16]{0:T(128)} %param.22) | copy-start | bytes 196
  10.7 13.2 %copy-start.31 = (f32[16]{0:T(128)S(1)}, f32[16]{0:T(128)}, u32[]{:S(2)}) copy-start(f32[16]{0:T(128)} %param.21) | copy-start | bytes 196
  11.5 17.3 %copy-start.6 = (bf16[256,2176]{1,0:T(8,128)(2,1)}, bf16[256,2176]{1,0:T(8,128)(2,1)S(1)}, u32[]{:S(2)}) copy-start(bf16[256,2176]{1,0:T(8,128)(2,1)S(1)} %convolution_convert_fusion) | copy-start | bytes 3342340
  12.3 25.7 %collective-permute-start.1 = (bf16[2,3,1152]{2,0,1:T(2,128)(2,1)}, bf16[2,3,1152]{2,0,1:T(2,128)(2,1)}, u32[]{:S(2)}, u32[]{:S(2)}) collective-permute-start(bf16[2,3,1152]{2,0,1:T(2,128)(2,1)} %copy.82), channel_id=1, source_target_pairs={{32,0},{64,32},{96,64},{128,96},{160,128},{192,160},{224,192},{256... | collective-permute-start | bytes 41480 | tf_op jit(solution)/shard_map/ppermute | solution.py:27
  21.6 23.7 %collective-permute-start = (bf16[2,3,1152]{2,0,1:T(2,128)(2,1)}, bf16[2,3,1152]{2,0,1:T(2,128)(2,1)}, u32[]{:S(2)}, u32[]{:S(2)}) collective-permute-start(bf16[2,3,1152]{2,0,1:T(2,128)(2,1)} %copy.79), channel_id=1, source_target_pairs={{0,32},{32,64},{64,96},{96,128},{128,160},{160,192},{192,224},{224... | collective-permute-start | bytes 41480 | tf_op jit(solution)/shard_map/ppermute | solution.py:25
  29.7 7.7 %copy-start.18 = (f32[2,128,16]{2,1,0:T(8,128)S(1)}, f32[2,128,16]{2,1,0:T(8,128)}, u32[]{:S(2)}) copy-start(f32[2,128,16]{2,1,0:T(8,128)} %get-tuple-element.376) | copy-start | bytes 49156
  47.2 6.5 %copy-start.26 = (f32[2,128,16]{1,2,0:T(8,128)S(1)}, f32[2,128,16]{1,2,0:T(8,128)}, u32[]{:S(2)}) copy-start(f32[2,128,16]{1,2,0:T(8,128)} %copy.59) | copy-start | bytes 49156
  47.2 6.5 %copy-start.30 = (f32[2,16]{1,0:T(2,128)S(1)}, f32[2,16]{1,0:T(2,128)}, u32[]{:S(2)}) copy-start(f32[2,16]{1,0:T(2,128)} %exponential_multiply_fusion.1) | copy-start | bytes 388
  52.7 5.4 %copy-start.1 = (bf16[2,128,1152]{1,2,0:T(8,128)(2,1)}, bf16[2,128,1152]{1,2,0:T(8,128)(2,1)S(1)}, u32[]{:S(2)}) copy-start(bf16[2,128,1152]{1,2,0:T(8,128)(2,1)S(1)} %get-tuple-element.377) | copy-start | bytes 1769476
  52.7 4.1 %copy-start.19 = (bf16[2,128,1024]{1,2,0:T(8,128)(2,1)}, bf16[2,128,1024]{1,2,0:T(8,128)(2,1)S(1)}, u32[]{:S(2)}) copy-start(bf16[2,128,1024]{1,2,0:T(8,128)(2,1)S(1)} %slice.133) | copy-start | bytes 1572868
  56.9 217.2 %all-gather.9.cloned.1.call-start = ((), (), s32[]{:S(2)}) async-start(), calls=%async_computation.1 | async-start | bytes 17825792 | tf_op jit(solution)/shard_map/all_gather | solution.py:59
  64.6 11.3 %copy-start.32 = (f32[16]{0:T(128)S(1)}, f32[16]{0:T(128)}, u32[]{:S(2)}) copy-start(f32[16]{0:T(128)} %param.23) | copy-start | bytes 196
  201.4 2.0 copy-start.17
  201.4 2.0 copy-start.20
  201.4 2.0 copy-start.24
  201.4 2.0 copy-start.25
  201.4 2.0 copy-start.27
  309.7 2.0 copy-start.13
  309.7 2.0 copy-start.16
  309.8 2.0 copy-start.22
  309.8 2.0 copy-start.23
  309.8 2.0 copy-start.28
  311.8 1.2 copy-start.4
  311.8 1.4 copy-start.5
  311.8 1.5 copy-start.10
  311.8 1.9 copy-start.15
  322.0 1.6 copy-start.9
  (7 other events, 6.9 us)
Sparse Core Ops, SparseCore 0:
  57.0 90.6 all-gather.6
  150.9 123.0 all-gather.8
where the time goes:
time: 335 us; the launch traced here: 331 us
  other arithmetic  88.8 us (27%)
  waiting for transfers between devices  84 us (25%)
  local copies, waits for them, and re-layouts  69.8 us (21%)
  blocking collectives  43.9 us (13%)
  matrix products  19.8 us (6%)
  between operations  13.9 us (4%)
  starting transfers between devices  10.7 us (3%)
    all_gather x1, waiting for transfers between devices, prefix_2(): everything = jax.tree.map(lambda part: lax.all_gather(part, axis), shard)  68.6 us
    select_n x32, other arithmetic, turn(): return jax.tree.map(lambda a, b: jnp.where(reached, a, b), new, before)  64.4 us
    all_gather x1, blocking collectives, prefix_2(): everything = jax.tree.map(lambda part: lax.all_gather(part, axis), shard)  23.7 us
    all_gather x1, blocking collectives, prefix(): lax.all_gather(part.astype(kind), axis)  20.2 us
    all_gather x1, waiting for transfers between devices, prefix(): lax.all_gather(part.astype(kind), axis)  15.3 us
    exp x16, local copies, waits for them, and re-layouts, chain_join(): jnp.exp(log_late)[:, :, None, None] * state_early + state_late  10.6 us
    slice x2, local copies, waits for them, and re-layouts, run_chain(): projected[:, :E]  10.5 us
    unnamed x76, local copies, waits for them, and re-layouts  10.2 us
  transfers between devices with their start and end apart: 4, of which 2 were waited for; matrix products, arithmetic and copies ran while one was open for 33% of the time, Pallas kernels for 0%

commit v1 on v0

v1 whole, which is shorter than its diff:
```python
import jax
import jax.numpy as jnp
from jax import lax
from jax.experimental import pallas as pl
from jax.experimental.pallas import tpu as pltpu
from jax.sharding import PartitionSpec as P

D = 512
E = 1024
N = 64
K = 4
BLOCK = 128
HEADS = 16
MIX = E + 2 * N
COUNT = 16
HALO = 16
EPS = 1e-05
LOG2E = 1.4426950408889634

F32 = jnp.float32
BF16 = jnp.bfloat16


def dot(a, b):
    return jnp.dot(a, b, preferred_element_type=F32)


def iota(shape, dim):
    return lax.broadcasted_iota(jnp.int32, shape, dim)


def ones_where(mask):
    return jnp.where(mask, 1.0, 0.0).astype(BF16)


def parts_of(x):
    hi = x.astype(BF16)
    rest = x - hi.astype(F32)
    mid = rest.astype(BF16)
    low = (rest - mid.astype(F32)).astype(BF16)
    return hi, mid, low


def split(x):
    hi, mid, low = parts_of(x)
    group = iota(x.shape, 1) // HEADS
    picked = jnp.where(
        group == 0,
        hi.astype(F32),
        jnp.where(group == 1, mid.astype(F32), jnp.where(group == 2, low.astype(F32), 0.0)),
    )
    return picked.astype(BF16)


def exact(values, ones):
    hi, mid, low = parts_of(values)
    return dot(hi, ones) + dot(mid, ones) + dot(low, ones)


def silu(x):
    return x / (1.0 + jnp.exp(-x))


def kernel(
    hidden,
    norm_gain,
    weight_hbm,
    step_weight,
    conv_weight,
    conv_bias,
    step_bias,
    log_rate,
    skip_gain,
    gate_gain,
    out_weight_hbm,
    out,
    weight,
    out_weight,
    out_flipped,
    halo,
    normal,
    ext,
    act,
    silu_gate,
    inside,
    ecum,
    state_out,
    state_in,
    decay_out,
    decay_in,
    mem_out,
    mem_in,
    expand64,
    expand128,
    load_sem,
    halo_send,
    halo_recv,
    state_send,
    state_recv,
    decay_send,
    decay_recv,
    mem_send,
    mem_recv,
):
    me = lax.axis_index("seq")
    load_w = pltpu.make_async_copy(weight_hbm, weight, load_sem.at[0])
    load_o = pltpu.make_async_copy(out_weight_hbm, out_weight, load_sem.at[1])
    load_w.start()
    load_o.start()

    barrier = pltpu.get_barrier_semaphore()
    for k in range(1, COUNT):
        pl.semaphore_signal(
            barrier,
            inc=1,
            device_id={"seq": lax.rem(me + k, COUNT)},
            device_id_type=pl.DeviceIdType.MESH,
        )

    flip = ones_where(iota((D, D), 0) + iota((D, D), 1) == D - 1)
    rows = iota((BLOCK, E), 0)
    expand64[...] = ones_where((rows % HEADS == iota((BLOCK, E), 1) // 64) & (rows < 3 * HEADS))
    wide = (BLOCK, HEADS * BLOCK)
    rows = iota(wide, 0)
    expand128[...] = ones_where((rows % HEADS == iota(wide, 1) // BLOCK) & (rows < 3 * HEADS))
    tile = ones_where(iota((HEADS, BLOCK), 1) % HEADS == iota((HEADS, BLOCK), 0))
    square = (BLOCK, BLOCK)
    lower = iota(square, 0) >= iota(square, 1)
    upper = iota(square, 0) <= iota(square, 1)
    shift = ones_where(iota(square, 0) == iota(square, 1) + N)
    gain = norm_gain[...]

    def normals(raw):
        floats = raw.astype(F32)
        scale = lax.rsqrt(jnp.mean(floats * floats, axis=-1, keepdims=True) + EPS)
        turned = dot(raw, flip)
        return (floats * scale * gain).astype(BF16), (turned * scale * gain).astype(BF16)

    straight, turned = normals(hidden[...])
    normal[0:BLOCK, :] = straight
    normal[BLOCK : 2 * BLOCK, :] = turned

    step_tiled = dot(step_weight[...], tile).astype(BF16)
    bias = exact(jnp.broadcast_to(step_bias[...], (8, HEADS)), tile)[0:1]
    rate = jnp.exp(exact(jnp.broadcast_to(log_rate[...], (8, HEADS)), tile)[0:1])
    raw = dot(normal[...], step_tiled) + bias
    soft = jnp.maximum(raw, 0.0) + jnp.log1p(jnp.exp(-jnp.abs(raw)))
    log_decay = -rate * soft

    pl.semaphore_wait(barrier, COUNT - 1)
    to_right = pltpu.make_async_remote_copy(
        src_ref=hidden.at[pl.ds(BLOCK - HALO, HALO)],
        dst_ref=halo.at[0],
        send_sem=halo_send.at[0],
        recv_sem=halo_recv.at[0],
        device_id={"seq": lax.rem(me + 1, COUNT)},
        device_id_type=pl.DeviceIdType.MESH,
    )
    to_left = pltpu.make_async_remote_copy(
        src_ref=hidden.at[pl.ds(0, HALO)],
        dst_ref=halo.at[1],
        send_sem=halo_send.at[1],
        recv_sem=halo_recv.at[1],
        device_id={"seq": lax.rem(me + COUNT - 1, COUNT)},
        device_id_type=pl.DeviceIdType.MESH,
    )
    to_right.start()
    to_left.start()

    load_w.wait()
    for c in range(0, MIX, 384):
        cols = slice(c, c + 384)
        mixed = dot(normal[...], weight[:, E + c : E + c + 384]).astype(BF16).astype(F32)
        ext[0, HALO : HALO + BLOCK, cols] = mixed[:BLOCK]
        ext[1, HALO : HALO + BLOCK, cols] = mixed[BLOCK:]

    to_right.wait()
    to_left.wait()
    left_rows = jnp.where(me == 0, 0.0, halo[0].astype(F32))
    right_rows = jnp.where(me == COUNT - 1, 0.0, halo[1].astype(F32))
    rim = jnp.concatenate([left_rows, right_rows], axis=0).astype(BF16)
    rim_normals = jnp.concatenate(normals(rim), axis=0)
    for c in range(0, MIX, 384):
        cols = slice(c, c + 384)
        mixed = dot(rim_normals, weight[:, E + c : E + c + 384]).astype(BF16).astype(F32)
        for j in range(2):
            ext[j, 0:HALO, cols] = mixed[2 * HALO * j : 2 * HALO * j + HALO]
            ext[j, HALO + BLOCK : 2 * HALO + BLOCK, cols] = mixed[
                2 * HALO * j + HALO : 2 * HALO * (j + 1)
            ]

    for c in range(MIX // 128):
        cols = slice(128 * c, 128 * c + 128)
        taps = [conv_weight[k : k + 1, cols] for k in range(K)]
        start = conv_bias[:, cols]
        for j in range(2):
            views = [ext[j, HALO - 3 + r : HALO - 3 + r + BLOCK, cols] for r in range(7)]
            ahead = start
            behind = start
            for k in range(K):
                ahead = ahead + taps[k] * views[k]
                behind = behind + taps[k] * views[6 - k]
            act[j, :, cols] = silu(ahead).astype(BF16)
            act[2 + j, :, cols] = silu(behind).astype(BF16)

    logs = []
    for chain in range(4):
        j, reverse = chain % 2, chain >= 2
        hi, mid, low = parts_of(log_decay[BLOCK * j : BLOCK * (j + 1)])
        tri = ones_where(upper if reverse else lower)
        cumulated = dot(tri, hi) + dot(tri, mid) + dot(tri, low)
        cumulated = cumulated * LOG2E
        last = cumulated[0:1] if reverse else cumulated[BLOCK - 1 : BLOCK]
        logs.append(cumulated)
        if not reverse:
            decay_out[j] = jnp.broadcast_to(jnp.exp2(last), (8, BLOCK))
        tail = split(jnp.exp2(last - cumulated))
        ecum[chain] = split(jnp.exp2(cumulated))
        both = act[chain, :, E:]
        for c in range(0, E, 256):
            cols = slice(c, c + 256)
            factor = dot(tail, expand64[:, cols])
            decayed = (factor * act[chain, :, cols].astype(F32)).astype(BF16)
            state = lax.dot_general(
                both, decayed, (((0,), (0,)), ((), ())), preferred_element_type=F32
            )
            for q in range(4):
                state_out[4 * chain + q, :, cols] = state[16 * q : 16 * q + 16].astype(BF16)

    def state_copy(target, slot):
        return pltpu.make_async_remote_copy(
            src_ref=state_out.at[target],
            dst_ref=state_in.at[slot],
            send_sem=state_send.at[target],
            recv_sem=state_recv.at[slot],
            device_id={"seq": target},
            device_id_type=pl.DeviceIdType.MESH,
        )

    def decay_copy(target, slot):
        return pltpu.make_async_remote_copy(
            src_ref=decay_out.at[lax.rem(target // 4, 2)],
            dst_ref=decay_in.at[slot],
            send_sem=decay_send.at[target],
            recv_sem=decay_recv.at[slot],
            device_id={"seq": target},
            device_id_type=pl.DeviceIdType.MESH,
        )

    def mem_copy(target, slot):
        return pltpu.make_async_remote_copy(
            src_ref=mem_out.at[target],
            dst_ref=mem_in.at[slot],
            send_sem=mem_send.at[target],
            recv_sem=mem_recv.at[slot],
            device_id={"seq": target},
            device_id_type=pl.DeviceIdType.MESH,
        )

    for k in range(1, COUNT):
        target = lax.rem(me + k, COUNT)
        state_copy(target, me).start()
        decay_copy(target, me).start()
    state_in[me] = state_out[me]
    decay_in[me] = decay_out[lax.rem(me // 4, 2)]

    for c in range(0, E, 256):
        cols = slice(c, c + 256)
        gate = dot(normal[...], weight[:, cols]).astype(BF16).astype(F32)
        silu_gate[:, cols] = silu(gate)
    load_o.wait()
    for r in range(0, E, 256):
        out_flipped[r : r + 256, :] = dot(out_weight[r : r + 256, :], flip).astype(BF16)
    repeat = ones_where(iota((HEADS, E), 1) // 64 == iota((HEADS, E), 0))
    skip = exact(jnp.broadcast_to(skip_gain[...], (8, HEADS)), repeat)[0:1]
    first = ones_where(iota(square, 1) < 64)
    second = ones_where(iota(square, 1) >= 64)
    for chain in range(4):
        reverse = chain >= 2
        columns = split(logs[chain])
        by_head = logs[chain].T
        both = act[chain, :, E:]
        reader = dot(both, shift).astype(BF16)
        scores = lax.dot_general(
            reader, both, (((1,), (1,)), ((), ())), preferred_element_type=F32
        )
        scores = jnp.where(upper if reverse else lower, scores, 0.0)
        scores = jnp.concatenate([scores, scores], axis=1)
        for p in range(HEADS // 2):
            cols = slice(128 * p, 128 * p + 128)
            at = dot(columns, expand128[:, 256 * p : 256 * p + 256])
            since = jnp.concatenate(
                [by_head[2 * p : 2 * p + 1], by_head[2 * p + 1 : 2 * p + 2]], axis=1
            )
            weights = (jnp.exp2(jnp.minimum(at - since, 0.0)) * scores).astype(BF16)
            signal = act[chain, :, cols]
            pair = jnp.concatenate([signal * first, signal * second], axis=0)
            inside[chain, :, cols] = dot(weights, pair) + skip[:, cols] * signal.astype(F32)

    onward = me < COUNT // 2
    for k in range(1, COUNT):
        other = lax.rem(me + k, COUNT)
        decay_copy(other, other).wait()
    grouped = decay_in[:, 0, :]
    spread = dot(split(grouped), expand64[...])
    carry = jnp.zeros((16, E), F32)
    for k in range(COUNT):
        source = jnp.where(onward, k, COUNT - 1 - k)
        mem_out[source] = carry.astype(BF16)

        @pl.when(source != me)
        def _():
            state_copy(source, source).wait()
            mem_copy(source, me).start()

        factor = jnp.where(onward, spread[k : k + 1], spread[COUNT - 1 - k : COUNT - k])
        carry = factor * carry + state_in[source].astype(F32)
    mem_in[me] = mem_out[me]
    for k in range(1, COUNT):
        other = lax.rem(me + k, COUNT)
        mem_copy(other, other).wait()

    results = []
    for chain in range(4):
        j = chain % 2
        reader = dot(act[chain, :, E:], shift).astype(BF16)[:, :N]
        memory = mem_in[4 * chain : 4 * chain + 4].reshape(N, E)
        total = jnp.zeros((BLOCK, 1), F32)
        for c in range(0, E, 256):
            cols = slice(c, c + 256)
            carried = dot(reader, memory[:, cols])
            scale = dot(ecum[chain], expand64[:, cols])
            gated = (inside[chain, :, cols] + scale * carried) * silu_gate[
                BLOCK * j : BLOCK * (j + 1), cols
            ]
            total = total + jnp.sum(gated * gated, axis=1, keepdims=True)
            inside[chain, :, cols] = gated
        scale = lax.rsqrt(total / E + EPS)
        final = (inside[chain] * scale * gate_gain[...]).astype(BF16)
        results.append(dot(final, out_weight[...] if j == 0 else out_flipped[...]))
    backward = (results[2] + results[3]).astype(BF16).astype(F32)
    out[...] = (results[0] + results[1] + backward).astype(BF16)


def on_device(
    hidden,
    norm_gain,
    input_weight,
    step_weight,
    conv_weight,
    conv_bias,
    step_bias,
    log_rate,
    skip_gain,
    gate_gain,
    output_weight,
):
    vmem = pl.BlockSpec(memory_space=pltpu.VMEM)
    anywhere = pl.BlockSpec(memory_space=pl.ANY)
    dma = pltpu.SemaphoreType.DMA
    return pl.pallas_call(
        kernel,
        out_shape=jax.ShapeDtypeStruct((BLOCK, D), BF16),
        in_specs=[vmem, vmem, anywhere] + [vmem] * 7 + [anywhere],
        out_specs=vmem,
        scratch_shapes=[
            pltpu.VMEM((D, E + MIX), BF16),
            pltpu.VMEM((E, D), BF16),
            pltpu.VMEM((E, D), BF16),
            pltpu.VMEM((2, HALO, D), BF16),
            pltpu.VMEM((2 * BLOCK, D), BF16),
            pltpu.VMEM((2, BLOCK + 2 * HALO, MIX), F32),
            pltpu.VMEM((4, BLOCK, MIX), BF16),
            pltpu.VMEM((2 * BLOCK, E), F32),
            pltpu.VMEM((4, BLOCK, E), F32),
            pltpu.VMEM((4, BLOCK, BLOCK), BF16),
            pltpu.VMEM((COUNT, 16, E), BF16),
            pltpu.VMEM((COUNT, 16, E), BF16),
            pltpu.VMEM((2, 8, BLOCK), F32),
            pltpu.VMEM((COUNT, 8, BLOCK), F32),
            pltpu.VMEM((COUNT, 16, E), BF16),
            pltpu.VMEM((COUNT, 16, E), BF16),
            pltpu.VMEM((BLOCK, E), BF16),
            pltpu.VMEM((BLOCK, HEADS * BLOCK), BF16),
            dma((2,)),
            dma((2,)),
            dma((2,)),
            dma((COUNT,)),
            dma((COUNT,)),
            dma((COUNT,)),
            dma((COUNT,)),
            dma((COUNT,)),
            dma((COUNT,)),
        ],
        compiler_params=pltpu.CompilerParams(
            collective_id=0, has_side_effects=True, vmem_limit_bytes=48 * 1024 * 1024
        ),
    )(
        hidden,
        norm_gain[None],
        input_weight,
        step_weight,
        conv_weight,
        conv_bias[None],
        step_bias[None],
        log_rate[None],
        skip_gain[None],
        gate_gain[None],
        output_weight,
    )


def solution(mesh):
    in_specs = (P(("batch", "seq"), None), P(), P(), P(), P(), P(), P(), P(), P(), P(), P())
    out_specs = P(("batch", "seq"), None)
    return jax.shard_map(
        on_device, mesh=mesh, in_specs=in_specs, out_specs=out_specs, check_vma=False
    )
```

time: 335 us -> 50.4 us (0.15); the launches traced: 331 us -> 50 us
  other arithmetic: 88.8 us -> 0 us
  waiting for transfers between devices: 84 us -> 0 us
  local copies, waits for them, and re-layouts: 69.8 us -> 10 us
  blocking collectives: 43.9 us -> 0 us
  Pallas kernels: 0 us -> 40 us
  matrix products: 19.8 us -> 0 us
  between operations: 13.9 us -> 0.03 us
  starting transfers between devices: 10.7 us -> 0 us
    all_gather x2 -> x0, waiting for transfers between devices: 83.9 us -> none  [the longest x1 68.6 us: prefix_2(): everything = jax.tree.map(lambda part: lax.all_gather(part, axis), shard)]
    select_n x32 -> x0, other arithmetic: 64.4 us -> none  [turn(): return jax.tree.map(lambda a, b: jnp.where(reached, a, b), new, before)]
    all_gather x2 -> x0, blocking collectives: 43.9 us -> none  [the longest x1 23.7 us: prefix_2(): everything = jax.tree.map(lambda part: lax.all_gather(part, axis), shard)]
    pallas_call x0 -> x1, Pallas kernels: none -> 40 us  [on_device(): pl.pallas_call(kernel, out_shape=jax.ShapeDtypeStruct((BLOCK, D), BF16),...]
    slice x11 -> x0, local copies, waits for them, and re-layouts: 19.9 us -> none  [the longest x2 10.5 us: run_chain(): projected[:, :E]]
    exp x20 -> x0, local copies, waits for them, and re-layouts: 14.5 us -> none  [the longest x16 10.6 us: chain_join(): jnp.exp(log_late)[:, :, None, None] * state_early + state_late]
    exp x18 -> x0, other arithmetic: 11.6 us -> none  [the longest x16 10.2 us: chain_join(): jnp.exp(log_late)[:, :, None, None] * state_early + state_late]
    dot_general x10 -> x0, matrix products: 11.1 us -> none  [the longest x2 2.88 us: block_step(): jnp.einsum('hts,shp->thp', weights, heads_x, preferred_element_type=jnp.f...]
  transfers between devices with their start and end apart: 4 -> 0, of which waited for: 2 -> 0; matrix products, arithmetic and copies ran while one was open for 33% -> 0% of each run, Pallas kernels for 0% -> 0%
where the time goes in v1:
time: 50.4 us; the launch traced here: 50 us
  Pallas kernels  40 us (79%)
  local copies, waits for them, and re-layouts  10 us (20%)
    pallas_call x1, Pallas kernels, on_device(): pl.pallas_call(kernel, out_shape=jax.ShapeDtypeStruct((BLOCK, D), BF16),...  40 us
    unnamed x20, local copies, waits for them, and re-layouts  9.3 us

profile of v1, /device:TPU:1, one launch (start us, length us, event | category | flops | bytes accessed | tf_op | source)
XLA Modules:
  0.0 50.0 jit_solution(7536793976044769818)
XLA Ops:
  0.0 0.7 %broadcast_in_dim.19.conv_bias = f32[1,1152]{1,0:T(1,128)S(1)} reshape(f32[1152]{0:T(1024)} %param.16) | data formatting | bytes 9216 | tf_op jit(solution)/shard_map/broadcast_in_dim | solution.py:404
  0.7 0.8 %copy.12.step_weight = bf16[512,16]{1,0:T(8,128)(2,1)S(1)} copy(bf16[512,16]{0,1:T(8,128)(2,1)} %param.14) | data formatting | bytes 32768 | tf_op args[3]
  1.5 0.0 copy-start
  1.6 1.6 %copy-done = bf16[512,2176]{1,0:T(8,128)(2,1)S(1)} copy-done((bf16[512,2176]{1,0:T(8,128)(2,1)S(1)}, bf16[512,2176]{1,0:T(8,128)(2,1)}, u32[]{:S(2)}) %copy-start) | copy-done | bytes 2228248
  3.2 0.0 copy-start.1
  3.2 1.2 %copy-done.1 = bf16[1024,512]{1,0:T(8,128)(2,1)S(1)} copy-done((bf16[1024,512]{1,0:T(8,128)(2,1)S(1)}, bf16[1024,512]{1,0:T(8,128)(2,1)}, u32[]{:S(2)}) %copy-start.1) | copy-done | bytes 1048600
  4.4 0.0 copy-start.2
  4.4 0.9 %copy-done.2 = bf16[128,512]{1,0:T(8,128)(2,1)S(1)} copy-done((bf16[128,512]{1,0:T(8,128)(2,1)S(1)}, bf16[128,512]{1,0:T(8,128)(2,1)}, u32[]{:S(2)}) %copy-start.2) | copy-done | bytes 131096
  5.3 0.0 copy-start.3
  5.3 0.7 %copy-done.3 = f32[4,1152]{1,0:T(4,128)S(1)} copy-done((f32[4,1152]{1,0:T(4,128)S(1)}, f32[4,1152]{1,0:T(4,128)}, u32[]{:S(2)}) %copy-start.3) | copy-done | bytes 18456
  6.0 0.0 copy-start.4
  6.0 0.7 %copy-done.4 = f32[1024]{0:T(1024)S(1)} copy-done((f32[1024]{0:T(1024)S(1)}, f32[1024]{0:T(1024)}, u32[]{:S(2)}) %copy-start.4) | copy-done | bytes 4120
  6.7 0.0 copy-start.5
  6.7 0.7 %copy-done.5 = f32[512]{0:T(512)S(1)} copy-done((f32[512]{0:T(512)S(1)}, f32[512]{0:T(512)}, u32[]{:S(2)}) %copy-start.5) | copy-done | bytes 2072
  7.4 0.0 copy-start.6
  7.4 0.7 %copy-done.6 = f32[16]{0:T(128)S(1)} copy-done((f32[16]{0:T(128)S(1)}, f32[16]{0:T(128)}, u32[]{:S(2)}) %copy-start.6) | copy-done | bytes 88
  8.1 0.0 copy-start.7
  8.1 0.7 %copy-done.7 = f32[16]{0:T(128)S(1)} copy-done((f32[16]{0:T(128)S(1)}, f32[16]{0:T(128)}, u32[]{:S(2)}) %copy-start.7) | copy-done | bytes 88
  8.7 0.0 copy-start.8
  8.7 0.7 %copy-done.8 = f32[16]{0:T(128)S(1)} copy-done((f32[16]{0:T(128)S(1)}, f32[16]{0:T(128)}, u32[]{:S(2)}) %copy-start.8) | copy-done | bytes 88
  9.4 40.0 %shard_map.109 = bf16[128,512]{1,0:T(8,128)(2,1)S(1)} custom-call(bf16[128,512]{1,0:T(8,128)(2,1)S(1)} %copy-done.2, f32[1,512]{1,0:T(1,128)S(1)} %bitcast.6, bf16[512,2176]{1,0:T(8,128)(2,1)S(1)} %copy-done, bf16[512,16]{1,0:T(8,128)(2,1)S(1)} %copy.12.step_weight, f32[4,1152]{1,0:T(4,128)S(1)} %copy-done.3, f32[1,1152]{1,0:T(1,128)S(1)} %broadcast_in_dim.19.conv_bias, ...), custom_call_target="tpu_custom_call" | custom-call | tf_op jit(solution)/shard_map/pallas_call | solution.py:361
  49.3 0.7 %copy.14 = bf16[128,512]{1,0:T(8,128)(2,1)} copy(bf16[128,512]{1,0:T(8,128)(2,1)S(1)} %shard_map.109) | data formatting | bytes 262144
Async XLA Ops:
  1.5 1.6 %copy-start = (bf16[512,2176]{1,0:T(8,128)(2,1)S(1)}, bf16[512,2176]{1,0:T(8,128)(2,1)}, u32[]{:S(2)}) copy-start(bf16[512,2176]{1,0:T(8,128)(2,1)} %weight_hbm.1) | copy-start | bytes 6684676
  3.2 1.2 %copy-start.1 = (bf16[1024,512]{1,0:T(8,128)(2,1)S(1)}, bf16[1024,512]{1,0:T(8,128)(2,1)}, u32[]{:S(2)}) copy-start(bf16[1024,512]{1,0:T(8,128)(2,1)} %out_weight_hbm.1) | copy-start | bytes 3145732
  4.4 0.9 %copy-start.2 = (bf16[128,512]{1,0:T(8,128)(2,1)S(1)}, bf16[128,512]{1,0:T(8,128)(2,1)}, u32[]{:S(2)}) copy-start(bf16[128,512]{1,0:T(8,128)(2,1)} %hidden.1) | copy-start | bytes 393220
  5.3 0.7 %copy-start.3 = (f32[4,1152]{1,0:T(4,128)S(1)}, f32[4,1152]{1,0:T(4,128)}, u32[]{:S(2)}) copy-start(f32[4,1152]{1,0:T(4,128)} %conv_weight.1) | copy-start | bytes 55300
  6.0 0.7 %copy-start.4 = (f32[1024]{0:T(1024)S(1)}, f32[1024]{0:T(1024)}, u32[]{:S(2)}) copy-start(f32[1024]{0:T(1024)} %param.20) | copy-start | bytes 12292
  6.7 0.7 %copy-start.5 = (f32[512]{0:T(512)S(1)}, f32[512]{0:T(512)}, u32[]{:S(2)}) copy-start(f32[512]{0:T(512)} %param.12) | copy-start | bytes 6148
  7.4 0.7 %copy-start.6 = (f32[16]{0:T(128)S(1)}, f32[16]{0:T(128)}, u32[]{:S(2)}) copy-start(f32[16]{0:T(128)} %param.17) | copy-start | bytes 196
  8.1 0.7 %copy-start.7 = (f32[16]{0:T(128)S(1)}, f32[16]{0:T(128)}, u32[]{:S(2)}) copy-start(f32[16]{0:T(128)} %param.18) | copy-start | bytes 196
  8.7 0.7 %copy-start.8 = (f32[16]{0:T(128)S(1)}, f32[16]{0:T(128)}, u32[]{:S(2)}) copy-start(f32[16]{0:T(128)} %param.19) | copy-start | bytes 196

commit v2 on v1

--- a/solution.py
+++ b/solution.py
@@ -62,9 +62,20 @@
 
 
 def kernel(
+    hidden_hbm,
+    norm_gain_hbm,
+    weight_hbm,
+    step_weight_hbm,
+    conv_weight_hbm,
+    conv_bias_hbm,
+    step_bias_hbm,
+    log_rate_hbm,
+    skip_gain_hbm,
+    gate_gain_hbm,
+    out_weight_hbm,
+    out,
     hidden,
     norm_gain,
-    weight_hbm,
     step_weight,
     conv_weight,
     conv_bias,
@@ -72,8 +83,6 @@
     log_rate,
     skip_gain,
     gate_gain,
-    out_weight_hbm,
-    out,
     weight,
     out_weight,
     out_flipped,
@@ -103,10 +112,24 @@
     mem_recv,
 ):
     me = lax.axis_index("seq")
-    load_w = pltpu.make_async_copy(weight_hbm, weight, load_sem.at[0])
-    load_o = pltpu.make_async_copy(out_weight_hbm, out_weight, load_sem.at[1])
-    load_w.start()
-    load_o.start()
+    moves = [
+        (hidden_hbm, hidden),
+        (norm_gain_hbm, norm_gain),
+        (step_weight_hbm, step_weight),
+        (step_bias_hbm, step_bias),
+        (log_rate_hbm, log_rate),
+        (weight_hbm.at[:, pl.ds(E, MIX)], weight.at[:, pl.ds(E, MIX)]),
+        (conv_weight_hbm, conv_weight),
+        (conv_bias_hbm, conv_bias),
+        (weight_hbm.at[:, pl.ds(0, E)], weight.at[:, pl.ds(0, E)]),
+        (skip_gain_hbm, skip_gain),
+        (out_weight_hbm, out_weight),
+        (gate_gain_hbm, gate_gain),
+    ]
+    loads = [
+        pltpu.make_async_copy(source, target, load_sem.at[i])
+        for i, (source, target) in enumerate(moves)
+    ]
 
     barrier = pltpu.get_barrier_semaphore()
     for k in range(1, COUNT):
@@ -116,6 +139,8 @@
             device_id={"seq": lax.rem(me + k, COUNT)},
             device_id_type=pl.DeviceIdType.MESH,
         )
+    for load in loads:
+        load.start()
 
     flip = ones_where(iota((D, D), 0) + iota((D, D), 1) == D - 1)
     rows = iota((BLOCK, E), 0)
@@ -128,6 +153,8 @@
     lower = iota(square, 0) >= iota(square, 1)
     upper = iota(square, 0) <= iota(square, 1)
     shift = ones_where(iota(square, 0) == iota(square, 1) + N)
+    loads[0].wait()
+    loads[1].wait()
     gain = norm_gain[...]
 
     def normals(raw):
@@ -140,10 +167,16 @@
     normal[0:BLOCK, :] = straight
     normal[BLOCK : 2 * BLOCK, :] = turned
 
-    step_tiled = dot(step_weight[...], tile).astype(BF16)
+    for load in loads[2:5]:
+        load.wait()
+    step_tiled = lax.dot_general(
+        tile, step_weight[...], (((0,), (0,)), ((), ())), preferred_element_type=F32
+    ).astype(BF16)
     bias = exact(jnp.broadcast_to(step_bias[...], (8, HEADS)), tile)[0:1]
     rate = jnp.exp(exact(jnp.broadcast_to(log_rate[...], (8, HEADS)), tile)[0:1])
-    raw = dot(normal[...], step_tiled) + bias
+    raw = bias + lax.dot_general(
+        normal[...], step_tiled, (((1,), (1,)), ((), ())), preferred_element_type=F32
+    )
     soft = jnp.maximum(raw, 0.0) + jnp.log1p(jnp.exp(-jnp.abs(raw)))
     log_decay = -rate * soft
 
@@ -167,7 +200,7 @@
     to_right.start()
     to_left.start()
 
-    load_w.wait()
+    loads[5].wait()
     for c in range(0, MIX, 384):
         cols = slice(c, c + 384)
         mixed = dot(normal[...], weight[:, E + c : E + c + 384]).astype(BF16).astype(F32)
@@ -189,10 +222,12 @@
                 2 * HALO * j + HALO : 2 * HALO * (j + 1)
             ]
 
+    loads[6].wait()
+    loads[7].wait()
     for c in range(MIX // 128):
         cols = slice(128 * c, 128 * c + 128)
         taps = [conv_weight[k : k + 1, cols] for k in range(K)]
-        start = conv_bias[:, cols]
+        start = conv_bias[cols][None, :]
         for j in range(2):
             views = [ext[j, HALO - 3 + r : HALO - 3 + r + BLOCK, cols] for r in range(7)]
             ahead = start
@@ -202,6 +237,36 @@
                 behind = behind + taps[k] * views[6 - k]
             act[j, :, cols] = silu(ahead).astype(BF16)
             act[2 + j, :, cols] = silu(behind).astype(BF16)
+
+    def state_copy(target, slot):
+        return pltpu.make_async_remote_copy(
+            src_ref=state_out.at[target],
+            dst_ref=state_in.at[slot],
+            send_sem=state_send.at[target],
+            recv_sem=state_recv.at[slot],
+            device_id={"seq": target},
+            device_id_type=pl.DeviceIdType.MESH,
+        )
+
+    def decay_copy(target, slot):
+        return pltpu.make_async_remote_copy(
+            src_ref=decay_out.at[lax.rem(target, 2)],
+            dst_ref=decay_in.at[slot],
+            send_sem=decay_send.at[target],
+            recv_sem=decay_recv.at[slot],
+            device_id={"seq": target},
+            device_id_type=pl.DeviceIdType.MESH,
+        )
+
+    def mem_copy(target, slot):
+        return pltpu.make_async_remote_copy(
+            src_ref=mem_out.at[target],
+            dst_ref=mem_in.at[slot],
+            send_sem=mem_send.at[target],
+            recv_sem=mem_recv.at[slot],
+            device_id={"seq": target},
+            device_id_type=pl.DeviceIdType.MESH,
+        )
 
     logs = []
     for chain in range(4):
@@ -225,50 +290,26 @@
                 both, decayed, (((0,), (0,)), ((), ())), preferred_element_type=F32
             )
             for q in range(4):
-                state_out[4 * chain + q, :, cols] = state[16 * q : 16 * q + 16].astype(BF16)
-
-    def state_copy(target, slot):
-        return pltpu.make_async_remote_copy(
-            src_ref=state_out.at[target],
-            dst_ref=state_in.at[slot],
-            send_sem=state_send.at[target],
-            recv_sem=state_recv.at[slot],
-            device_id={"seq": target},
-            device_id_type=pl.DeviceIdType.MESH,
-        )
-
-    def decay_copy(target, slot):
-        return pltpu.make_async_remote_copy(
-            src_ref=decay_out.at[lax.rem(target // 4, 2)],
-            dst_ref=decay_in.at[slot],
-            send_sem=decay_send.at[target],
-            recv_sem=decay_recv.at[slot],
-            device_id={"seq": target},
-            device_id_type=pl.DeviceIdType.MESH,
-        )
-
-    def mem_copy(target, slot):
-        return pltpu.make_async_remote_copy(
-            src_ref=mem_out.at[target],
-            dst_ref=mem_in.at[slot],
-            send_sem=mem_send.at[target],
-            recv_sem=mem_recv.at[slot],
-            device_id={"seq": target},
-            device_id_type=pl.DeviceIdType.MESH,
-        )
-
-    for k in range(1, COUNT):
-        target = lax.rem(me + k, COUNT)
-        state_copy(target, me).start()
-        decay_copy(target, me).start()
+                state_out[4 * q + chain, :, cols] = state[16 * q : 16 * q + 16].astype(BF16)
+        for q in range(4):
+            target = lax.rem(me + 4 * q, COUNT) // 4 * 4 + chain
+
+            @pl.when(target != me)
+            def _():
+                state_copy(target, me).start()
+                decay_copy(target, me).start()
+
     state_in[me] = state_out[me]
-    decay_in[me] = decay_out[lax.rem(me // 4, 2)]
-
+    decay_in[me] = decay_out[lax.rem(me, 2)]
+
+    loads[8].wait()
     for c in range(0, E, 256):
         cols = slice(c, c + 256)
         gate = dot(normal[...], weight[:, cols]).astype(BF16).astype(F32)
         silu_gate[:, cols] = silu(gate)
-    load_o.wait()
+    loads[9].wait()
+    loads[10].wait()
+    loads[11].wait()
     for r in range(0, E, 256):
         out_flipped[r : r + 256, :] = dot(out_weight[r : r + 256, :], flip).astype(BF16)
     repeat = ones_where(iota((HEADS, E), 1) // 64 == iota((HEADS, E), 0))
@@ -297,7 +338,7 @@
             pair = jnp.concatenate([signal * first, signal * second], axis=0)
             inside[chain, :, cols] = dot(weights, pair) + skip[:, cols] * signal.astype(F32)
 
-    onward = me < COUNT // 2
+    onward = lax.rem(me, 4) < 2
     for k in range(1, COUNT):
         other = lax.rem(me + k, COUNT)
         decay_copy(other, other).wait()
@@ -316,15 +357,18 @@
         factor = jnp.where(onward, spread[k : k + 1], spread[COUNT - 1 - k : COUNT - k])
         carry = factor * carry + state_in[source].astype(F32)
     mem_in[me] = mem_out[me]
-    for k in range(1, COUNT):
-        other = lax.rem(me + k, COUNT)
-        mem_copy(other, other).wait()
-
     results = []
     for chain in range(4):
         j = chain % 2
+        for q in range(4):
+            owner = 4 * q + chain
+
+            @pl.when(owner != me)
+            def _():
+                mem_copy(owner, owner).wait()
+
         reader = dot(act[chain, :, E:], shift).astype(BF16)[:, :N]
-        memory = mem_in[4 * chain : 4 * chain + 4].reshape(N, E)
+        memory = jnp.concatenate([mem_in[4 * q + chain] for q in range(4)], axis=0)
         total = jnp.zeros((BLOCK, 1), F32)
         for c in range(0, E, 256):
             cols = slice(c, c + 256)
@@ -356,14 +400,22 @@
     output_weight,
 ):
     vmem = pl.BlockSpec(memory_space=pltpu.VMEM)
-    anywhere = pl.BlockSpec(memory_space=pl.ANY)
     dma = pltpu.SemaphoreType.DMA
     return pl.pallas_call(
         kernel,
         out_shape=jax.ShapeDtypeStruct((BLOCK, D), BF16),
-        in_specs=[vmem, vmem, anywhere] + [vmem] * 7 + [anywhere],
+        in_specs=[pl.BlockSpec(memory_space=pltpu.HBM)] * 11,
         out_specs=vmem,
         scratch_shapes=[
+            pltpu.VMEM((BLOCK, D), BF16),
+            pltpu.VMEM((1, D), F32),
+            pltpu.VMEM((HEADS, D), BF16),
+            pltpu.VMEM((K, MIX), F32),
+            pltpu.VMEM((MIX,), F32),
+            pltpu.VMEM((1, HEADS), F32),
+            pltpu.VMEM((1, HEADS), F32),
+            pltpu.VMEM((1, HEADS), F32),
+            pltpu.VMEM((1, E), F32),
             pltpu.VMEM((D, E + MIX), BF16),
             pltpu.VMEM((E, D), BF16),
             pltpu.VMEM((E, D), BF16),
@@ -382,9 +434,9 @@
             pltpu.VMEM((COUNT, 16, E), BF16),
             pltpu.VMEM((BLOCK, E), BF16),
             pltpu.VMEM((BLOCK, HEADS * BLOCK), BF16),
+            dma((12,)),
             dma((2,)),
             dma((2,)),
-            dma((2,)),
             dma((COUNT,)),
             dma((COUNT,)),
             dma((COUNT,)),
@@ -393,15 +445,15 @@
             dma((COUNT,)),
         ],
         compiler_params=pltpu.CompilerParams(
-            collective_id=0, has_side_effects=True, vmem_limit_bytes=48 * 1024 * 1024
+            collective_id=0, has_side_effects=True, vmem_limit_bytes=60 * 1024 * 1024
         ),
     )(
         hidden,
         norm_gain[None],
         input_weight,
-        step_weight,
+        step_weight.T,
         conv_weight,
-        conv_bias[None],
+        conv_bias,
         step_bias[None],
         log_rate[None],
         skip_gain[None],

time: 50.4 us -> 40.5 us (0.80)
  local copies, waits for them, and re-layouts: 10 us -> 1.57 us
  Pallas kernels: 40 us -> 38.8 us
    unnamed x20 -> x1, local copies, waits for them, and re-layouts: 9.3 us -> 1.57 us
    pallas_call x1, Pallas kernels: 40 us -> 38.8 us  [on_device(): pl.pallas_call(kernel, out_shape=jax.ShapeDtypeStruct((BLOCK, D), BF16),...]
    broadcast_in_dim x1 -> x0, local copies, waits for them, and re-layouts: 0.7 us -> none  [on_device(): conv_bias[None]]
where the time goes in v2:
time: 40.5 us; the launch traced here: 40.4 us
  Pallas kernels  38.8 us (96%)
  local copies, waits for them, and re-layouts  1.57 us (4%)
    pallas_call x1, Pallas kernels, on_device(): pl.pallas_call(kernel, out_shape=jax.ShapeDtypeStruct((BLOCK, D), BF16),...  38.8 us
    unnamed x1, local copies, waits for them, and re-layouts  1.57 us

profile of v2, /device:TPU:1, one launch (start us, length us, event | category | flops | bytes accessed | tf_op | source)
XLA Modules:
  0.0 40.4 jit_solution(14393974130254272407)
XLA Ops:
  0.0 38.8 %shard_map.109 = bf16[128,512]{1,0:T(8,128)(2,1)} custom-call(bf16[128,512]{1,0:T(8,128)(2,1)} %hidden_hbm.1, f32[1,512]{1,0:T(1,128)} %bitcast.8, bf16[512,2176]{1,0:T(8,128)(2,1)} %weight_hbm.1, bf16[16,512]{1,0:T(8,128)(2,1)} %bitcast.6, f32[4,1152]{1,0:T(4,128)} %conv_weight_hbm.1, f32[1152]{0:T(1024)} %conv_bias_hbm.1, f32[1,16]{1,0:T(1,128)} %bitcast.9, ...), custom_call_target="tpu_custom_call" | custom-call | tf_op jit(solution)/shard_map/pallas_call | solution.py:404
  38.8 1.6 %copy.13 = bf16[128,512]{1,0:T(8,128)(2,1)} copy(bf16[128,512]{1,0:T(8,128)(2,1)} %shard_map.109) | data formatting | bytes 262144

commit v3 on v2

--- a/solution.py
+++ b/solution.py
@@ -93,25 +93,37 @@
     silu_gate,
     inside,
     ecum,
-    state_out,
-    state_in,
+    tails,
+    cums,
+    pair_out,
+    pair_in,
     decay_out,
     decay_in,
+    sum_out,
+    sum_in,
     mem_out,
     mem_in,
+    cross_out,
+    cross_in,
     expand64,
     expand128,
     load_sem,
     halo_send,
     halo_recv,
-    state_send,
-    state_recv,
     decay_send,
     decay_recv,
+    pair_send,
+    pair_recv,
+    sum_send,
+    sum_recv,
     mem_send,
     mem_recv,
+    cross_send,
+    cross_recv,
 ):
     me = lax.axis_index("seq")
+    chip, core = me // 2, lax.rem(me, 2)
+    partner = me + 1 - 2 * core
     moves = [
         (hidden_hbm, hidden),
         (norm_gain_hbm, norm_gain),
@@ -179,6 +191,22 @@
     )
     soft = jnp.maximum(raw, 0.0) + jnp.log1p(jnp.exp(-jnp.abs(raw)))
     log_decay = -rate * soft
+    lasts = []
+    for chain in range(4):
+        j, reverse = chain % 2, chain >= 2
+        hi, mid, low = parts_of(log_decay[BLOCK * j : BLOCK * (j + 1)])
+        tri = ones_where(upper if reverse else lower)
+        cumulated = (dot(tri, hi) + dot(tri, mid) + dot(tri, low)) * LOG2E
+        last = cumulated[0:1] if reverse else cumulated[BLOCK - 1 : BLOCK]
+        if not reverse:
+            lasts.append(jnp.exp2(last))
+        cums[chain] = cumulated
+        tails[chain] = split(jnp.exp2(last - cumulated))
+        ecum[chain] = split(jnp.exp2(cumulated))
+    top = iota((8, BLOCK), 0) == 0
+    decays = jnp.where(top, lasts[0], lasts[1])
+    decay_out[...] = decays
+    decay_in[me] = decays
 
     pl.semaphore_wait(barrier, COUNT - 1)
     to_right = pltpu.make_async_remote_copy(
@@ -200,6 +228,59 @@
     to_right.start()
     to_left.start()
 
+    def decay_copy(target, slot):
+        return pltpu.make_async_remote_copy(
+            src_ref=decay_out,
+            dst_ref=decay_in.at[slot],
+            send_sem=decay_send.at[target],
+            recv_sem=decay_recv.at[slot],
+            device_id={"seq": target},
+            device_id_type=pl.DeviceIdType.MESH,
+        )
+
+    def pair_copy(j):
+        return pltpu.make_async_remote_copy(
+            src_ref=pair_out.at[2 * (1 - core) + j],
+            dst_ref=pair_in.at[j],
+            send_sem=pair_send.at[j],
+            recv_sem=pair_recv.at[j],
+            device_id={"seq": partner},
+            device_id_type=pl.DeviceIdType.MESH,
+        )
+
+    def sum_copy(target, slot):
+        return pltpu.make_async_remote_copy(
+            src_ref=sum_out.at[target],
+            dst_ref=sum_in.at[slot],
+            send_sem=sum_send.at[target],
+            recv_sem=sum_recv.at[slot],
+            device_id={"seq": 2 * target + core},
+            device_id_type=pl.DeviceIdType.MESH,
+        )
+
+    def mem_copy(target, slot):
+        return pltpu.make_async_remote_copy(
+            src_ref=mem_out.at[target],
+            dst_ref=mem_in.at[slot],
+            send_sem=mem_send.at[target],
+            recv_sem=mem_recv.at[slot],
+            device_id={"seq": 2 * target + core},
+            device_id_type=pl.DeviceIdType.MESH,
+        )
+
+    def cross_copy(j):
+        return pltpu.make_async_remote_copy(
+            src_ref=cross_out.at[j],
+            dst_ref=cross_in.at[j],
+            send_sem=cross_send.at[j],
+            recv_sem=cross_recv.at[j],
+            device_id={"seq": partner},
+            device_id_type=pl.DeviceIdType.MESH,
+        )
+
+    for k in range(1, COUNT):
+        decay_copy(lax.rem(me + k, COUNT), me).start()
+
     loads[5].wait()
     for c in range(0, MIX, 384):
         cols = slice(c, c + 384)
@@ -238,69 +319,36 @@
             act[j, :, cols] = silu(ahead).astype(BF16)
             act[2 + j, :, cols] = silu(behind).astype(BF16)
 
-    def state_copy(target, slot):
-        return pltpu.make_async_remote_copy(
-            src_ref=state_out.at[target],
-            dst_ref=state_in.at[slot],
-            send_sem=state_send.at[target],
-            recv_sem=state_recv.at[slot],
-            device_id={"seq": target},
-            device_id_type=pl.DeviceIdType.MESH,
-        )
-
-    def decay_copy(target, slot):
-        return pltpu.make_async_remote_copy(
-            src_ref=decay_out.at[lax.rem(target, 2)],
-            dst_ref=decay_in.at[slot],
-            send_sem=decay_send.at[target],
-            recv_sem=decay_recv.at[slot],
-            device_id={"seq": target},
-            device_id_type=pl.DeviceIdType.MESH,
-        )
-
-    def mem_copy(target, slot):
-        return pltpu.make_async_remote_copy(
-            src_ref=mem_out.at[target],
-            dst_ref=mem_in.at[slot],
-            send_sem=mem_send.at[target],
-            recv_sem=mem_recv.at[slot],
-            device_id={"seq": target},
-            device_id_type=pl.DeviceIdType.MESH,
-        )
-
-    logs = []
-    for chain in range(4):
-        j, reverse = chain % 2, chain >= 2
-        hi, mid, low = parts_of(log_decay[BLOCK * j : BLOCK * (j + 1)])
-        tri = ones_where(upper if reverse else lower)
-        cumulated = dot(tri, hi) + dot(tri, mid) + dot(tri, low)
-        cumulated = cumulated * LOG2E
-        last = cumulated[0:1] if reverse else cumulated[BLOCK - 1 : BLOCK]
-        logs.append(cumulated)
-        if not reverse:
-            decay_out[j] = jnp.broadcast_to(jnp.exp2(last), (8, BLOCK))
-        tail = split(jnp.exp2(last - cumulated))
-        ecum[chain] = split(jnp.exp2(cumulated))
+    for chain, j in [(2 * (1 - core) + j, j) for j in range(2)] + [(2 * core + j, None) for j in range(2)]:
         both = act[chain, :, E:]
         for c in range(0, E, 256):
             cols = slice(c, c + 256)
-            factor = dot(tail, expand64[:, cols])
+            factor = dot(tails[chain], expand64[:, cols])
             decayed = (factor * act[chain, :, cols].astype(F32)).astype(BF16)
             state = lax.dot_general(
                 both, decayed, (((0,), (0,)), ((), ())), preferred_element_type=F32
             )
-            for q in range(4):
-                state_out[4 * q + chain, :, cols] = state[16 * q : 16 * q + 16].astype(BF16)
+            pair_out[chain, :, cols] = state[:N].astype(BF16)
+        if j is not None:
+            pair_copy(j).start()
+
+    for k in range(1, COUNT):
+        other = lax.rem(me + k, COUNT)
+        decay_copy(other, other).wait()
+    near = [dot(split(decay_in[d]), expand64[...]) for d in (me, partner)]
+    for j in range(2):
+        pair_copy(j).wait()
+        joined = near[1][j : j + 1] * pair_out[2 * core + j].astype(F32) + pair_in[j].astype(F32)
+        joined = joined.astype(BF16)
         for q in range(4):
-            target = lax.rem(me + 4 * q, COUNT) // 4 * 4 + chain
-
-            @pl.when(target != me)
+            sum_out[4 * j + q] = joined[16 * q : 16 * q + 16]
+        for q in range(4):
+            target = 4 * j + lax.rem(chip + q, 4)
+
+            @pl.when(target != chip)
             def _():
-                state_copy(target, me).start()
-                decay_copy(target, me).start()
-
-    state_in[me] = state_out[me]
-    decay_in[me] = decay_out[lax.rem(me, 2)]
+                sum_copy(target, chip).start()
+    sum_in[chip] = sum_out[chip]
 
     loads[8].wait()
     for c in range(0, E, 256):
@@ -318,8 +366,8 @@
     second = ones_where(iota(square, 1) >= 64)
     for chain in range(4):
         reverse = chain >= 2
-        columns = split(logs[chain])
-        by_head = logs[chain].T
+        columns = split(cums[chain])
+        by_head = cums[chain].T
         both = act[chain, :, E:]
         reader = dot(both, shift).astype(BF16)
         scores = lax.dot_general(
@@ -338,37 +386,29 @@
             pair = jnp.concatenate([signal * first, signal * second], axis=0)
             inside[chain, :, cols] = dot(weights, pair) + skip[:, cols] * signal.astype(F32)
 
-    onward = lax.rem(me, 4) < 2
-    for k in range(1, COUNT):
-        other = lax.rem(me + k, COUNT)
-        decay_copy(other, other).wait()
-    grouped = decay_in[:, 0, :]
-    spread = dot(split(grouped), expand64[...])
+    mine = jnp.where(chip < 4, decay_in[:, 0, :], decay_in[:, 1, :])
+    spread = dot(split(mine), expand64[...])
     carry = jnp.zeros((16, E), F32)
-    for k in range(COUNT):
-        source = jnp.where(onward, k, COUNT - 1 - k)
+    for k in range(COUNT // 2):
+        back = COUNT // 2 - 1 - k
+        source = jnp.where(core == 0, k, back)
         mem_out[source] = carry.astype(BF16)
 
-        @pl.when(source != me)
+        @pl.when(source != chip)
         def _():
-            state_copy(source, source).wait()
-            mem_copy(source, me).start()
-
-        factor = jnp.where(onward, spread[k : k + 1], spread[COUNT - 1 - k : COUNT - k])
-        carry = factor * carry + state_in[source].astype(F32)
-    mem_in[me] = mem_out[me]
-    results = []
-    for chain in range(4):
-        j = chain % 2
-        for q in range(4):
-            owner = 4 * q + chain
-
-            @pl.when(owner != me)
-            def _():
-                mem_copy(owner, owner).wait()
-
+            sum_copy(source, source).wait()
+            mem_copy(source, chip).start()
+
+        factor = jnp.where(
+            core == 0,
+            spread[2 * k : 2 * k + 1] * spread[2 * k + 1 : 2 * k + 2],
+            spread[2 * back : 2 * back + 1] * spread[2 * back + 1 : 2 * back + 2],
+        )
+        carry = factor * carry + sum_in[source].astype(F32)
+    mem_in[chip] = mem_out[chip]
+
+    def finish(chain, j, memory):
         reader = dot(act[chain, :, E:], shift).astype(BF16)[:, :N]
-        memory = jnp.concatenate([mem_in[4 * q + chain] for q in range(4)], axis=0)
         total = jnp.zeros((BLOCK, 1), F32)
         for c in range(0, E, 256):
             cols = slice(c, c + 256)
@@ -381,9 +421,30 @@
             inside[chain, :, cols] = gated
         scale = lax.rsqrt(total / E + EPS)
         final = (inside[chain] * scale * gate_gain[...]).astype(BF16)
-        results.append(dot(final, out_weight[...] if j == 0 else out_flipped[...]))
-    backward = (results[2] + results[3]).astype(BF16).astype(F32)
-    out[...] = (results[0] + results[1] + backward).astype(BF16)
+        return dot(final, out_weight[...] if j == 0 else out_flipped[...])
+
+    memories = []
+    for j in range(2):
+        for q in range(4):
+            owner = 4 * j + q
+
+            @pl.when(owner != chip)
+            def _():
+                mem_copy(owner, owner).wait()
+
+        memory = jnp.concatenate([mem_in[4 * j + q] for q in range(4)], axis=0)
+        onward = near[0][j : j + 1] * memory.astype(F32) + pair_out[2 * core + j].astype(F32)
+        cross_out[j] = onward.astype(BF16)
+        cross_copy(j).start()
+        memories.append(memory)
+    own = finish(2 * core, 0, memories[0]) + finish(2 * core + 1, 1, memories[1])
+    other = jnp.zeros((BLOCK, D), F32)
+    for j in range(2):
+        cross_copy(j).wait()
+        other = other + finish(2 * (1 - core) + j, j, cross_in[j])
+    forward = jnp.where(core == 0, own, other)
+    backward = jnp.where(core == 0, other, own).astype(BF16).astype(F32)
+    out[...] = (forward + backward).astype(BF16)
 
 
 def on_device(
@@ -426,12 +487,18 @@
             pltpu.VMEM((2 * BLOCK, E), F32),
             pltpu.VMEM((4, BLOCK, E), F32),
             pltpu.VMEM((4, BLOCK, BLOCK), BF16),
-            pltpu.VMEM((COUNT, 16, E), BF16),
-            pltpu.VMEM((COUNT, 16, E), BF16),
-            pltpu.VMEM((2, 8, BLOCK), F32),
+            pltpu.VMEM((4, BLOCK, BLOCK), BF16),
+            pltpu.VMEM((4, BLOCK, BLOCK), F32),
+            pltpu.VMEM((4, N, E), BF16),
+            pltpu.VMEM((2, N, E), BF16),
+            pltpu.VMEM((8, BLOCK), F32),
             pltpu.VMEM((COUNT, 8, BLOCK), F32),
-            pltpu.VMEM((COUNT, 16, E), BF16),
-            pltpu.VMEM((COUNT, 16, E), BF16),
+            pltpu.VMEM((COUNT // 2, 16, E), BF16),
+            pltpu.VMEM((COUNT // 2, 16, E), BF16),
+            pltpu.VMEM((COUNT // 2, 16, E), BF16),
+            pltpu.VMEM((COUNT // 2, 16, E), BF16),
+            pltpu.VMEM((2, N, E), BF16),
+            pltpu.VMEM((2, N, E), BF16),
             pltpu.VMEM((BLOCK, E), BF16),
             pltpu.VMEM((BLOCK, HEADS * BLOCK), BF16),
             dma((12,)),
@@ -439,10 +506,14 @@
             dma((2,)),
             dma((COUNT,)),
             dma((COUNT,)),
-            dma((COUNT,)),
-            dma((COUNT,)),
-            dma((COUNT,)),
-            dma((COUNT,)),
+            dma((2,)),
+            dma((2,)),
+            dma((COUNT // 2,)),
+            dma((COUNT // 2,)),
+            dma((COUNT // 2,)),
+            dma((COUNT // 2,)),
+            dma((2,)),
+            dma((2,)),
         ],
         compiler_params=pltpu.CompilerParams(
             collective_id=0, has_side_effects=True, vmem_limit_bytes=60 * 1024 * 1024

time: 40.5 us -> 36 us (0.89)
  Pallas kernels: 38.8 us -> 34.3 us
    pallas_call x1, Pallas kernels: 38.8 us -> 34.3 us  [on_device(): pl.pallas_call(kernel, out_shape=jax.ShapeDtypeStruct((BLOCK, D), BF16),...]
where the time goes in v3:
time: 36 us; the launch traced here: 35.9 us
  Pallas kernels  34.3 us (95%)
  local copies, waits for them, and re-layouts  1.57 us (4%)
    pallas_call x1, Pallas kernels, on_device(): pl.pallas_call(kernel, out_shape=jax.ShapeDtypeStruct((BLOCK, D), BF16),...  34.3 us
    unnamed x1, local copies, waits for them, and re-layouts  1.57 us

profile of v3, /device:TPU:1, one launch (start us, length us, event | category | flops | bytes accessed | tf_op | source)
XLA Modules:
  0.0 35.9 jit_solution(14315540083157281403)
XLA Ops:
  0.0 34.3 %shard_map.109 = bf16[128,512]{1,0:T(8,128)(2,1)} custom-call(bf16[128,512]{1,0:T(8,128)(2,1)} %hidden_hbm.1, f32[1,512]{1,0:T(1,128)} %bitcast.8, bf16[512,2176]{1,0:T(8,128)(2,1)} %weight_hbm.1, bf16[16,512]{1,0:T(8,128)(2,1)} %bitcast.6, f32[4,1152]{1,0:T(4,128)} %conv_weight_hbm.1, f32[1152]{0:T(1024)} %conv_bias_hbm.1, f32[1,16]{1,0:T(1,128)} %bitcast.9, ...), custom_call_target="tpu_custom_call" | custom-call | tf_op jit(solution)/shard_map/pallas_call | solution.py:465
  34.3 1.6 %copy.13 = bf16[128,512]{1,0:T(8,128)(2,1)} copy(bf16[128,512]{1,0:T(8,128)(2,1)} %shard_map.109) | data formatting | bytes 262144

commit v4 on v3

--- a/solution.py
+++ b/solution.py
@@ -143,6 +143,7 @@
         for i, (source, target) in enumerate(moves)
     ]
 
+    loads[0].start()
     barrier = pltpu.get_barrier_semaphore()
     for k in range(1, COUNT):
         pl.semaphore_signal(
@@ -151,7 +152,7 @@
             device_id={"seq": lax.rem(me + k, COUNT)},
             device_id_type=pl.DeviceIdType.MESH,
         )
-    for load in loads:
+    for load in loads[1:]:
         load.start()
 
     flip = ones_where(iota((D, D), 0) + iota((D, D), 1) == D - 1)
@@ -166,6 +167,26 @@
     upper = iota(square, 0) <= iota(square, 1)
     shift = ones_where(iota(square, 0) == iota(square, 1) + N)
     loads[0].wait()
+    pl.semaphore_wait(barrier, COUNT - 1)
+    to_right = pltpu.make_async_remote_copy(
+        src_ref=hidden.at[pl.ds(BLOCK - HALO, HALO)],
+        dst_ref=halo.at[0],
+        send_sem=halo_send.at[0],
+        recv_sem=halo_recv.at[0],
+        device_id={"seq": lax.rem(me + 1, COUNT)},
+        device_id_type=pl.DeviceIdType.MESH,
+    )
+    to_left = pltpu.make_async_remote_copy(
+        src_ref=hidden.at[pl.ds(0, HALO)],
+        dst_ref=halo.at[1],
+        send_sem=halo_send.at[1],
+        recv_sem=halo_recv.at[1],
+        device_id={"seq": lax.rem(me + COUNT - 1, COUNT)},
+        device_id_type=pl.DeviceIdType.MESH,
+    )
+    to_right.start()
+    to_left.start()
+
     loads[1].wait()
     gain = norm_gain[...]
 
@@ -207,26 +228,6 @@
     decays = jnp.where(top, lasts[0], lasts[1])
     decay_out[...] = decays
     decay_in[me] = decays
-
-    pl.semaphore_wait(barrier, COUNT - 1)
-    to_right = pltpu.make_async_remote_copy(
-        src_ref=hidden.at[pl.ds(BLOCK - HALO, HALO)],
-        dst_ref=halo.at[0],
-        send_sem=halo_send.at[0],
-        recv_sem=halo_recv.at[0],
-        device_id={"seq": lax.rem(me + 1, COUNT)},
-        device_id_type=pl.DeviceIdType.MESH,
-    )
-    to_left = pltpu.make_async_remote_copy(
-        src_ref=hidden.at[pl.ds(0, HALO)],
-        dst_ref=halo.at[1],
-        send_sem=halo_send.at[1],
-        recv_sem=halo_recv.at[1],
-        device_id={"seq": lax.rem(me + COUNT - 1, COUNT)},
-        device_id_type=pl.DeviceIdType.MESH,
-    )
-    to_right.start()
-    to_left.start()
 
     def decay_copy(target, slot):
         return pltpu.make_async_remote_copy(
@@ -516,7 +517,7 @@
             dma((2,)),
         ],
         compiler_params=pltpu.CompilerParams(
-            collective_id=0, has_side_effects=True, vmem_limit_bytes=60 * 1024 * 1024
+            collective_id=0, has_side_effects=True, vmem_limit_bytes=32 * 1024 * 1024
         ),
     )(
         hidden,

time: 36 us -> 44.8 us (1.24)
  local copies, waits for them, and re-layouts: 1.57 us -> 9.88 us
    unnamed x1 -> x23, local copies, waits for them, and re-layouts: 1.57 us -> 9.88 us
where the time goes in v4:
time: 44.8 us; the launch traced here: 44.4 us
  Pallas kernels  34.5 us (77%)
  local copies, waits for them, and re-layouts  9.88 us (22%)
    pallas_call x1, Pallas kernels, on_device(): pl.pallas_call(kernel, out_shape=jax.ShapeDtypeStruct((BLOCK, D), BF16),...  34.5 us
    unnamed x23, local copies, waits for them, and re-layouts  9.88 us

profile of v4, /device:TPU:1, one launch (start us, length us, event | category | flops | bytes accessed | tf_op | source)
XLA Modules:
  0.0 44.4 jit_solution(3734034106148486445)
XLA Ops:
  0.0 0.0 copy-start
  0.0 1.6 %copy-done = bf16[512,2176]{1,0:T(8,128)(2,1)S(1)} copy-done((bf16[512,2176]{1,0:T(8,128)(2,1)S(1)}, bf16[512,2176]{1,0:T(8,128)(2,1)}, u32[]{:S(2)}) %copy-start) | copy-done | bytes 2228248
  1.6 0.0 copy-start.1
  1.6 1.2 %copy-done.1 = bf16[1024,512]{1,0:T(8,128)(2,1)S(1)} copy-done((bf16[1024,512]{1,0:T(8,128)(2,1)S(1)}, bf16[1024,512]{1,0:T(8,128)(2,1)}, u32[]{:S(2)}) %copy-start.1) | copy-done | bytes 1048600
  2.9 0.0 copy-start.2
  2.9 0.9 %copy-done.2 = bf16[128,512]{1,0:T(8,128)(2,1)S(1)} copy-done((bf16[128,512]{1,0:T(8,128)(2,1)S(1)}, bf16[128,512]{1,0:T(8,128)(2,1)}, u32[]{:S(2)}) %copy-start.2) | copy-done | bytes 131096
  3.8 0.0 copy-start.3
  3.8 0.7 %copy-done.3 = f32[4,1152]{1,0:T(4,128)S(1)} copy-done((f32[4,1152]{1,0:T(4,128)S(1)}, f32[4,1152]{1,0:T(4,128)}, u32[]{:S(2)}) %copy-start.3) | copy-done | bytes 18456
  4.5 0.0 copy-start.4
  4.5 0.7 %copy-done.4 = bf16[512,16]{0,1:T(8,128)(2,1)S(1)} copy-done((bf16[512,16]{0,1:T(8,128)(2,1)S(1)}, bf16[512,16]{0,1:T(8,128)(2,1)}, u32[]{:S(2)}) %copy-start.4) | copy-done | bytes 16408
  5.2 0.0 copy-start.5
  5.2 0.7 %copy-done.5 = f32[1152]{0:T(1024)S(1)} copy-done((f32[1152]{0:T(1024)S(1)}, f32[1152]{0:T(1024)}, u32[]{:S(2)}) %copy-start.5) | copy-done | bytes 4632
  5.9 0.0 copy-start.6
  5.9 0.7 %copy-done.6 = f32[1024]{0:T(1024)S(1)} copy-done((f32[1024]{0:T(1024)S(1)}, f32[1024]{0:T(1024)}, u32[]{:S(2)}) %copy-start.6) | copy-done | bytes 4120
  6.6 0.0 copy-start.7
  6.6 0.7 %copy-done.7 = f32[512]{0:T(512)S(1)} copy-done((f32[512]{0:T(512)S(1)}, f32[512]{0:T(512)}, u32[]{:S(2)}) %copy-start.7) | copy-done | bytes 2072
  7.3 0.0 copy-start.8
  7.3 0.7 %copy-done.8 = f32[16]{0:T(128)S(1)} copy-done((f32[16]{0:T(128)S(1)}, f32[16]{0:T(128)}, u32[]{:S(2)}) %copy-start.8) | copy-done | bytes 88
  7.9 0.0 copy-start.9
  7.9 0.7 %copy-done.9 = f32[16]{0:T(128)S(1)} copy-done((f32[16]{0:T(128)S(1)}, f32[16]{0:T(128)}, u32[]{:S(2)}) %copy-start.9) | copy-done | bytes 88
  8.6 0.0 copy-start.10
  8.6 0.7 %copy-done.10 = f32[16]{0:T(128)S(1)} copy-done((f32[16]{0:T(128)S(1)}, f32[16]{0:T(128)}, u32[]{:S(2)}) %copy-start.10) | copy-done | bytes 88
  9.2 34.5 %shard_map.109 = bf16[128,512]{1,0:T(8,128)(2,1)S(1)} custom-call(bf16[128,512]{1,0:T(8,128)(2,1)S(1)} %copy-done.2, f32[1,512]{1,0:T(1,128)S(1)} %bitcast.8, bf16[512,2176]{1,0:T(8,128)(2,1)S(1)} %copy-done, bf16[16,512]{1,0:T(8,128)(2,1)S(1)} %bitcast.6, f32[4,1152]{1,0:T(4,128)S(1)} %copy-done.3, f32[1152]{0:T(1024)S(1)} %copy-done.5, ...), custom_call_target="tpu_custom_call" | custom-call | tf_op jit(solution)/shard_map/pallas_call | solution.py:466
  43.7 0.7 %copy.13 = bf16[128,512]{1,0:T(8,128)(2,1)} copy(bf16[128,512]{1,0:T(8,128)(2,1)S(1)} %shard_map.109) | data formatting | bytes 262144
Async XLA Ops:
  0.0 1.6 %copy-start = (bf16[512,2176]{1,0:T(8,128)(2,1)S(1)}, bf16[512,2176]{1,0:T(8,128)(2,1)}, u32[]{:S(2)}) copy-start(bf16[512,2176]{1,0:T(8,128)(2,1)} %weight_hbm.1) | copy-start | bytes 6684676
  1.6 1.2 %copy-start.1 = (bf16[1024,512]{1,0:T(8,128)(2,1)S(1)}, bf16[1024,512]{1,0:T(8,128)(2,1)}, u32[]{:S(2)}) copy-start(bf16[1024,512]{1,0:T(8,128)(2,1)} %out_weight_hbm.1) | copy-start | bytes 3145732
  2.9 0.9 %copy-start.2 = (bf16[128,512]{1,0:T(8,128)(2,1)S(1)}, bf16[128,512]{1,0:T(8,128)(2,1)}, u32[]{:S(2)}) copy-start(bf16[128,512]{1,0:T(8,128)(2,1)} %hidden_hbm.1) | copy-start | bytes 393220
  3.8 0.7 %copy-start.3 = (f32[4,1152]{1,0:T(4,128)S(1)}, f32[4,1152]{1,0:T(4,128)}, u32[]{:S(2)}) copy-start(f32[4,1152]{1,0:T(4,128)} %conv_weight_hbm.1) | copy-start | bytes 55300
  4.5 0.7 %copy-start.4 = (bf16[512,16]{0,1:T(8,128)(2,1)S(1)}, bf16[512,16]{0,1:T(8,128)(2,1)}, u32[]{:S(2)}) copy-start(bf16[512,16]{0,1:T(8,128)(2,1)} %param.14) | copy-start | bytes 49156
  5.2 0.7 %copy-start.5 = (f32[1152]{0:T(1024)S(1)}, f32[1152]{0:T(1024)}, u32[]{:S(2)}) copy-start(f32[1152]{0:T(1024)} %conv_bias_hbm.1) | copy-start | bytes 13828
  5.9 0.7 %copy-start.6 = (f32[1024]{0:T(1024)S(1)}, f32[1024]{0:T(1024)}, u32[]{:S(2)}) copy-start(f32[1024]{0:T(1024)} %param.20) | copy-start | bytes 12292
  6.6 0.7 %copy-start.7 = (f32[512]{0:T(512)S(1)}, f32[512]{0:T(512)}, u32[]{:S(2)}) copy-start(f32[512]{0:T(512)} %param.12) | copy-start | bytes 6148
  7.3 0.7 %copy-start.8 = (f32[16]{0:T(128)S(1)}, f32[16]{0:T(128)}, u32[]{:S(2)}) copy-start(f32[16]{0:T(128)} %param.17) | copy-start | bytes 196
  7.9 0.7 %copy-start.9 = (f32[16]{0:T(128)S(1)}, f32[16]{0:T(128)}, u32[]{:S(2)}) copy-start(f32[16]{0:T(128)} %param.18) | copy-start | bytes 196
  8.6 0.7 %copy-start.10 = (f32[16]{0:T(128)S(1)}, f32[16]{0:T(128)}, u32[]{:S(2)}) copy-start(f32[16]{0:T(128)} %param.19) | copy-start | bytes 196

commit v5 on v4

--- a/solution.py
+++ b/solution.py
@@ -92,6 +92,8 @@
     act,
     silu_gate,
     inside,
+    factors,
+    readers,
     ecum,
     tails,
     cums,
@@ -371,6 +373,8 @@
         by_head = cums[chain].T
         both = act[chain, :, E:]
         reader = dot(both, shift).astype(BF16)
+        readers[chain] = reader
+        gate_block = slice(BLOCK * (chain % 2), BLOCK * (chain % 2) + BLOCK)
         scores = lax.dot_general(
             reader, both, (((1,), (1,)), ((), ())), preferred_element_type=F32
         )
@@ -385,7 +389,10 @@
             weights = (jnp.exp2(jnp.minimum(at - since, 0.0)) * scores).astype(BF16)
             signal = act[chain, :, cols]
             pair = jnp.concatenate([signal * first, signal * second], axis=0)
-            inside[chain, :, cols] = dot(weights, pair) + skip[:, cols] * signal.astype(F32)
+            gate = silu_gate[gate_block, cols]
+            local = dot(weights, pair) + skip[:, cols] * signal.astype(F32)
+            inside[chain, :, cols] = local * gate
+            factors[chain, :, cols] = dot(ecum[chain], expand64[:, cols]) * gate
 
     mine = jnp.where(chip < 4, decay_in[:, 0, :], decay_in[:, 1, :])
     spread = dot(split(mine), expand64[...])
@@ -409,15 +416,12 @@
     mem_in[chip] = mem_out[chip]
 
     def finish(chain, j, memory):
-        reader = dot(act[chain, :, E:], shift).astype(BF16)[:, :N]
+        reader = readers[chain][:, :N]
         total = jnp.zeros((BLOCK, 1), F32)
         for c in range(0, E, 256):
             cols = slice(c, c + 256)
             carried = dot(reader, memory[:, cols])
-            scale = dot(ecum[chain], expand64[:, cols])
-            gated = (inside[chain, :, cols] + scale * carried) * silu_gate[
-                BLOCK * j : BLOCK * (j + 1), cols
-            ]
+            gated = inside[chain, :, cols] + factors[chain, :, cols] * carried
             total = total + jnp.sum(gated * gated, axis=1, keepdims=True)
             inside[chain, :, cols] = gated
         scale = lax.rsqrt(total / E + EPS)
@@ -487,6 +491,8 @@
             pltpu.VMEM((4, BLOCK, MIX), BF16),
             pltpu.VMEM((2 * BLOCK, E), F32),
             pltpu.VMEM((4, BLOCK, E), F32),
+            pltpu.VMEM((4, BLOCK, E), F32),
+            pltpu.VMEM((4, BLOCK, BLOCK), BF16),
             pltpu.VMEM((4, BLOCK, BLOCK), BF16),
             pltpu.VMEM((4, BLOCK, BLOCK), BF16),
             pltpu.VMEM((4, BLOCK, BLOCK), F32),
@@ -517,7 +523,7 @@
             dma((2,)),
         ],
         compiler_params=pltpu.CompilerParams(
-            collective_id=0, has_side_effects=True, vmem_limit_bytes=32 * 1024 * 1024
+            collective_id=0, has_side_effects=True, vmem_limit_bytes=60 * 1024 * 1024
         ),
     )(
         hidden,

time: 44.8 us -> 35.9 us (0.80)
  local copies, waits for them, and re-layouts: 9.88 us -> 1.57 us
    unnamed x23 -> x1, local copies, waits for them, and re-layouts: 9.88 us -> 1.57 us
where the time goes in v5:
time: 35.9 us; the launch traced here: 35.7 us
  Pallas kernels  34.2 us (95%)
  local copies, waits for them, and re-layouts  1.57 us (4%)
    pallas_call x1, Pallas kernels, on_device(): pl.pallas_call(kernel, out_shape=jax.ShapeDtypeStruct((BLOCK, D), BF16),...  34.2 us
    unnamed x1, local copies, waits for them, and re-layouts  1.57 us

profile of v5, /device:TPU:1, one launch (start us, length us, event | category | flops | bytes accessed | tf_op | source)
XLA Modules:
  0.0 35.7 jit_solution(14450994490398941217)
XLA Ops:
  0.0 34.2 %shard_map.109 = bf16[128,512]{1,0:T(8,128)(2,1)} custom-call(bf16[128,512]{1,0:T(8,128)(2,1)} %hidden_hbm.1, f32[1,512]{1,0:T(1,128)} %bitcast.8, bf16[512,2176]{1,0:T(8,128)(2,1)} %weight_hbm.1, bf16[16,512]{1,0:T(8,128)(2,1)} %bitcast.6, f32[4,1152]{1,0:T(4,128)} %conv_weight_hbm.1, f32[1152]{0:T(1024)} %conv_bias_hbm.1, f32[1,16]{1,0:T(1,128)} %bitcast.9, ...), custom_call_target="tpu_custom_call" | custom-call | tf_op jit(solution)/shard_map/pallas_call | solution.py:470
  34.2 1.6 %copy.13 = bf16[128,512]{1,0:T(8,128)(2,1)} copy(bf16[128,512]{1,0:T(8,128)(2,1)} %shard_map.109) | data formatting | bytes 262144

commit v6 on v5

--- a/solution.py
+++ b/solution.py
@@ -344,9 +344,10 @@
         joined = near[1][j : j + 1] * pair_out[2 * core + j].astype(F32) + pair_in[j].astype(F32)
         joined = joined.astype(BF16)
         for q in range(4):
-            sum_out[4 * j + q] = joined[16 * q : 16 * q + 16]
+            sum_out[2 * q + (q + j) % 2] = joined[16 * q : 16 * q + 16]
         for q in range(4):
-            target = 4 * j + lax.rem(chip + q, 4)
+            across = lax.rem(chip // 2 + q, 4)
+            target = 2 * across + lax.rem(across + j, 2)
 
             @pl.when(target != chip)
             def _():
@@ -394,7 +395,7 @@
             inside[chain, :, cols] = local * gate
             factors[chain, :, cols] = dot(ecum[chain], expand64[:, cols]) * gate
 
-    mine = jnp.where(chip < 4, decay_in[:, 0, :], decay_in[:, 1, :])
+    mine = jnp.where(lax.rem(chip // 2 + chip, 2) == 0, decay_in[:, 0, :], decay_in[:, 1, :])
     spread = dot(split(mine), expand64[...])
     carry = jnp.zeros((16, E), F32)
     for k in range(COUNT // 2):
@@ -431,13 +432,13 @@
     memories = []
     for j in range(2):
         for q in range(4):
-            owner = 4 * j + q
+            owner = 2 * q + (q + j) % 2
 
             @pl.when(owner != chip)
             def _():
                 mem_copy(owner, owner).wait()
 
-        memory = jnp.concatenate([mem_in[4 * j + q] for q in range(4)], axis=0)
+        memory = jnp.concatenate([mem_in[2 * q + (q + j) % 2] for q in range(4)], axis=0)
         onward = near[0][j : j + 1] * memory.astype(F32) + pair_out[2 * core + j].astype(F32)
         cross_out[j] = onward.astype(BF16)
         cross_copy(j).start()

time: 35.9 us -> 35.2 us (0.981)
  Pallas kernels: 34.2 us -> 33.5 us
    pallas_call x1, Pallas kernels: 34.2 us -> 33.5 us  [on_device(): pl.pallas_call(kernel, out_shape=jax.ShapeDtypeStruct((BLOCK, D), BF16),...]
where the time goes in v6:
time: 35.2 us; the launch traced here: 35 us
  Pallas kernels  33.5 us (95%)
  local copies, waits for them, and re-layouts  1.57 us (4%)
    pallas_call x1, Pallas kernels, on_device(): pl.pallas_call(kernel, out_shape=jax.ShapeDtypeStruct((BLOCK, D), BF16),...  33.5 us
    unnamed x1, local copies, waits for them, and re-layouts  1.57 us

profile of v6, /device:TPU:1, one launch (start us, length us, event | category | flops | bytes accessed | tf_op | source)
XLA Modules:
  0.0 35.0 jit_solution(11782601551200996397)
XLA Ops:
  0.0 33.5 %shard_map.109 = bf16[128,512]{1,0:T(8,128)(2,1)} custom-call(bf16[128,512]{1,0:T(8,128)(2,1)} %hidden_hbm.1, f32[1,512]{1,0:T(1,128)} %bitcast.8, bf16[512,2176]{1,0:T(8,128)(2,1)} %weight_hbm.1, bf16[16,512]{1,0:T(8,128)(2,1)} %bitcast.6, f32[4,1152]{1,0:T(4,128)} %conv_weight_hbm.1, f32[1152]{0:T(1024)} %conv_bias_hbm.1, f32[1,16]{1,0:T(1,128)} %bitcast.9, ...), custom_call_target="tpu_custom_call" | custom-call | tf_op jit(solution)/shard_map/pallas_call | solution.py:471
  33.5 1.6 %copy.13 = bf16[128,512]{1,0:T(8,128)(2,1)} copy(bf16[128,512]{1,0:T(8,128)(2,1)} %shard_map.109) | data formatting | bytes 262144
